TPU v7x, 256 devices: a whole 4x4x8 slice. The times are simulated.
256 devices in a mesh: head: 16 (over y_hi, z), ctx: 16 (over x, y_lo, core).
Axes of the slice: x: 4, y: 4 (y_hi: 2, y_lo: 2; y = y_hi * 2 + y_lo), z: 8, core: 2. Of those that a mesh axis runs over, the one named last changes fastest.
Arguments:
- queries: bfloat16 [8192, 2048], P(('ctx', 'head')), may hold values from -9 to 9
- keys: bfloat16 [8192, 8192], P('ctx', 'head'), may hold values from -9 to 9
- values: bfloat16 [8192, 8192], P('ctx', 'head'), may hold values from -6 to 6
- routes: int32 [8192, 16], P(('ctx', 'head')), may hold values from 0 to 63, all different within a row; in each aligned block of 32 rows (0 to 31, 32 to 63, ...) at most 16 rows name the same one
- gates: float32 [8192, 16], P(('ctx', 'head')), may hold values from 0.25 to 1
- block_mask: int32 [64, 64], replicated, may hold values 0 or 1
- w_out: bfloat16 [8192, 8192], P('head'), may hold values from -0.125 to 0.125
Outputs:
- mixed: bfloat16 [8192, 8192], P(('ctx', 'head'))
Inputs may be any that keep to these rules, and one draw needn't show every extreme that they name: `routes`: in each aligned block of 32 rows (the rows of one device) no head is named more than 16 times; each row names 16 different heads.
All inputs are finite; a program needn't handle non-finite values.
Results may differ from a plain program's by a relative error of at most 0.015.
Values may be sent and summed in bfloat16 or wider, within the bound.
No kernel may reach another device: no remote copies, remote signals or barrier semaphores. Data moves between devices by JAX's collectives and lax.ppermute only.
A program may use at most 128 MiB of HBM per device.

v0:
```python
import math

import jax
import jax.numpy as jnp
from jax import lax
from jax.experimental import pallas as pl
from jax.experimental.pallas import tpu as pltpu
from jax.sharding import PartitionSpec as P

H = 64
HD = 128
BLK = 128
CAP = 16
NX = 4
NJ = 4
NZ = 8
HALF = 2048
NEG = -1e30
SCALE2 = math.log2(math.e) / math.sqrt(HD)
BF = jnp.bfloat16
F32 = jnp.float32
NT = (((1,), (1,)), ((), ()))


def vmem():
    return pl.BlockSpec(memory_space=pltpu.VMEM)


def grant(mib):
    return pltpu.CompilerParams(vmem_limit_bytes=mib << 20)


def pack_kernel(q_ref, tgt_ref, gate_ref, out_ref):
    rows = jnp.concatenate([q_ref[:, k * HD : (k + 1) * HD] for k in range(16)], axis=0)
    tgt = tgt_ref[...]
    gate = gate_ref[...]
    hi = gate.astype(BF).astype(F32)
    mid = (gate - hi).astype(BF).astype(F32)
    tok = (lax.broadcasted_iota(jnp.int32, (1, 512), 1) % 32 + 1).astype(F32)
    aux = jnp.concatenate([tok, hi, mid, gate - hi - mid, jnp.zeros((12, 512), F32)], axis=0).astype(BF)
    for dest in range(16):
        slot = lax.broadcasted_iota(jnp.int32, (64, 512), 0) + dest * 64
        sel = jnp.where(slot == tgt, 1.0, 0.0).astype(BF)
        out_ref[dest, 0:64, :] = jnp.dot(sel, rows, preferred_element_type=F32).astype(BF)
        meta = lax.dot_general(aux, sel, NT, preferred_element_type=F32)
        meta = jnp.concatenate([meta, jnp.zeros((16, 64), F32)], axis=1)
        out_ref[dest, 64:80, :] = meta.astype(BF)


def attend_kernel(sets, flag_ref, bias_ref, lim_ref, *refs):
    count = len(sets)
    q_refs, kv_refs, out_refs = refs[:count], refs[count : count + 4], refs[count + 4 : 2 * count + 4]
    kv, sems, list_ref, done_ref, s_ref, m_ref, acc_ref = refs[2 * count + 4 :]
    copies = [pltpu.make_async_copy(src, kv.at[i], sems.at[i]) for i, src in enumerate(kv_refs)]
    for copy in copies:
        copy.start()
    copies[0].wait()
    done_ref[0] = jnp.int32(0)

    def keys_ready(last):
        for i in range(1, 4):

            @pl.when((last >= i) & (done_ref[0] < i))
            def _():
                copies[i].wait()
                done_ref[0] = jnp.int32(i)

    ones = jnp.ones((16, 256), BF)
    key_id = lax.broadcasted_iota(jnp.int32, (BLK, 256), 0).astype(F32)

    def two_blocks(q_ref, first, second, bias, lims):
        blocks = (first, second)
        state = {}

        def scores(p):
            q = q_ref[:, p * CAP : (p + 1) * CAP, :].reshape(256, HD)
            old = m_ref[p : p + 1, :]
            new = old
            for n, block in enumerate(blocks):
                k = kv[block // 4, pl.ds(pl.multiple_of((block % 4) * BLK, BLK), BLK), p * HD : (p + 1) * HD]
                s = lax.dot_general(k, q, NT, preferred_element_type=F32)
                if lims is not None:
                    s = jnp.where(key_id <= lims(p, n), s, 2.0 * NEG)
                s_ref[p, n * BLK : (n + 1) * BLK, :] = s
                top = jnp.max(s, axis=0, keepdims=True)
                new = jnp.maximum(new, top if bias is None else top + bias[n])
            m_ref[p : p + 1, :] = new
            state[p] = (new, jnp.exp2((old - new) * SCALE2))

        def values(p):
            new, factor = state[p]
            ws, vts = [], []
            for n, block in enumerate(blocks):
                base = new if bias is None else new - bias[n]
                ws.append(jnp.exp2((s_ref[p, n * BLK : (n + 1) * BLK, :] - base) * SCALE2).astype(BF))
                vts.append(kv[block // 4, 512 + p * HD : 512 + (p + 1) * HD, pl.ds(pl.multiple_of((block % 4) * BLK, BLK), BLK)])
            left = jnp.concatenate([jnp.concatenate(vts, axis=1), ones], axis=0)
            gain = jnp.dot(left, jnp.concatenate(ws, axis=0), preferred_element_type=F32)
            acc_ref[p * 144 : (p + 1) * 144, :] = acc_ref[p * 144 : (p + 1) * 144, :] * factor + gain

        scores(0)
        scores(1)
        values(0)
        scores(2)
        values(1)
        scores(3)
        values(2)
        values(3)

    for n, dx in enumerate(sets):
        q_ref, out_ref = q_refs[n], out_refs[n]
        m_ref[...] = jnp.full(m_ref.shape, NEG, F32)
        acc_ref[...] = jnp.zeros(acc_ref.shape, F32)
        if dx == 0:

            def diag_step(pair, _, q_ref=q_ref):
                def lims(p, n):
                    return lim_ref[pl.ds(p * 4 + pair * 2 + n, 1), :]

                two_blocks(q_ref, pair * 2, pair * 2 + 1, None, lims)
                return 0

            lax.fori_loop(0, 2, diag_step, 0)
        found = jnp.int32(0)
        for block in range(4 if dx == 0 else 0, 16):
            list_ref[found] = jnp.int32(block)
            found = found + flag_ref[dx, block]
        list_ref[found] = jnp.int32(16)

        def pair_step(pair, _, q_ref=q_ref, dx=dx, n=n):
            one, two = list_ref[pair * 2], list_ref[pair * 2 + 1]
            if n == 0:
                keys_ready(jnp.minimum(two, 15) // 4)
            bias = (bias_ref[pl.ds(dx * 24 + one, 1), :], bias_ref[pl.ds(dx * 24 + two, 1), :])
            two_blocks(q_ref, one, jnp.minimum(two, 15), bias, None)
            return 0

        lax.fori_loop(0, (found + 1) // 2, pair_step, 0)
        if n == 0:
            keys_ready(3)
        total = jnp.concatenate([acc_ref[p * 144 + HD : p * 144 + HD + 1, :] for p in range(4)], axis=0)
        some = total > 0.0
        safe = jnp.where(some, total, 1.0)
        inv = jnp.where(some, 1.0 / safe, 0.0)
        lse = jnp.where(some, m_ref[0:4, :] * SCALE2 + jnp.log2(safe), NEG)
        hi = lse.astype(BF)
        rest = lse - hi.astype(F32)
        mid = rest.astype(BF)
        low = (rest - mid.astype(F32)).astype(BF)
        for p in range(4):
            out_ref[p * HD : (p + 1) * HD, :] = (acc_ref[p * 144 : p * 144 + HD, :] * inv[p : p + 1, :]).astype(BF)
        out_ref[512:528, :] = jnp.concatenate([hi, mid, low, jnp.zeros((4, 256), BF)], axis=0)


def attend(sets, flags, bias, lim, qs, kvs):
    part = jax.ShapeDtypeStruct((528, 256), BF)
    return pl.pallas_call(
        lambda *refs: attend_kernel(sets, *refs),
        out_shape=[part] * len(sets),
        in_specs=[pl.BlockSpec(memory_space=pltpu.SMEM)]
        + [vmem()] * (2 + len(sets))
        + [pl.BlockSpec(memory_space=pl.ANY)] * 4,
        out_specs=[vmem()] * len(sets),
        scratch_shapes=[
            pltpu.VMEM((4, 1024, 512), BF),
            pltpu.SemaphoreType.DMA((4,)),
            pltpu.SMEM((18,), jnp.int32),
            pltpu.SMEM((1,), jnp.int32),
            pltpu.VMEM((4, 256, 256), F32),
            pltpu.VMEM((8, 256), F32),
            pltpu.VMEM((576, 256), F32),
        ],
        cost_estimate=pl.CostEstimate(
            flops=len(sets) * 2 * 2 * 4 * 256 * 2048 * 128,
            bytes_accessed=5 << 20,
            transcendentals=len(sets) * 4 * 256 * 2048,
        ),
        compiler_params=grant(24),
        name="attend",
    )(flags, bias, lim, *qs, *kvs)


def place_heads(heads, pos, out_ref, lo):
    token = lax.broadcasted_iota(jnp.int32, (256, HD), 0).astype(F32)
    for r in range(2):
        place = jnp.where(token + r * 256.0 == pos[:, r * HD : (r + 1) * HD], 1.0, 0.0).astype(BF)
        out_ref[r * 256 : (r + 1) * 256, lo : lo + HD] = lax.dot_general(
            place, heads[:, r * HD : (r + 1) * HD], NT, preferred_element_type=F32
        ).astype(BF)


def slot_pos(tok):
    dev = (lax.broadcasted_iota(jnp.int32, tok.shape, 1) // CAP).astype(F32)
    return jnp.where(tok >= 0.0, dev * 32.0 + tok, -1.0)


def merge_kernel(a_ref, b_ref, c_ref, d_ref, tok_ref, gate_ref, send_ref):
    parts = (a_ref, b_ref, c_ref, d_ref)
    lses = []
    for ref in parts:
        tail = ref[512:528, :].astype(F32)
        lses.append(tail[0:4] + tail[4:8] + tail[8:12])
    top = jnp.maximum(jnp.maximum(lses[0], lses[1]), jnp.maximum(lses[2], lses[3]))
    ws = [jnp.exp2(lse - top) for lse in lses]
    norm = gate_ref[...] / (ws[0] + ws[1] + ws[2] + ws[3])
    ws = [w * norm for w in ws]
    for p in range(4):
        mix = None
        for ref, w in zip(parts, ws):
            term = ref[p * HD : (p + 1) * HD, :].astype(F32) * w[p : p + 1, :]
            mix = term if mix is None else mix + term
        send_ref[p * HD : (p + 1) * HD, :] = mix.astype(BF)
    send_ref[512:528, :] = jnp.concatenate([tok_ref[...], jnp.zeros((12, 256), F32)], axis=0).astype(BF)


def place_kernel(sent_ref, out_ref):
    pos = slot_pos(sent_ref[512:528, :].astype(F32))
    for p in range(4):
        place_heads(sent_ref[p * HD : (p + 1) * HD, :], pos[p : p + 1, :], out_ref, p * HD)


def spread_kernel(core_ref, got_ref, out_ref):
    pos = slot_pos(got_ref[512:528, :].astype(F32))
    core = core_ref[0]
    for n in range(4):
        half = core if n < 2 else 1 - core
        q = n % 2
        start = pl.multiple_of(half * 256 + q * HD, HD)
        row = jnp.where(half == 0, pos[q : q + 1, :], pos[2 + q : 3 + q, :])
        place_heads(got_ref[pl.ds(start, HD), :], row, out_ref, n * HD)


def project_kernel(hops, place_ref, a_ref, b_ref, wa_ref, wb_ref, wc_ref, up0_ref, up_ref, down0_ref, down_ref, own_ref, total_ref):
    total = jnp.dot(a_ref[...], wa_ref[...], preferred_element_type=F32)
    total += jnp.dot(b_ref[:, 0:256], wb_ref[...], preferred_element_type=F32)
    total += jnp.dot(b_ref[:, 256:512], wc_ref[...], preferred_element_type=F32)
    total_ref[...] = total.astype(BF)
    z = place_ref[1]

    def rows(half, ahead):
        dest = (z + (ahead + NZ)) % NZ
        return total_ref[pl.ds(pl.multiple_of(half * 256 + dest * 32, 32), 32), :]

    for half in range(2):
        own_ref[half] = rows(half, 0)
        for step, length, first, rest in ((1, hops[0], up0_ref, up_ref), (-1, hops[1], down0_ref, down_ref)):
            first[half] = rows(half, step * length)
            for hop in range(1, length):
                rest[hop - 1, half] = rows(half, step * (length - hop))


TILE = 512
STEPS = HALF // TILE


def project(place, chunk, hops, a, b, w_out, wb, wc):
    def terms(*lead):
        return jax.ShapeDtypeStruct((*lead, 2, 32, HALF), BF)

    def block(*lead):
        zeros = (0,) * (len(lead) + 2)
        return pl.BlockSpec((*lead, 2, 32, TILE), lambda i, s: (*zeros, i))

    leads = ((), (hops[0] - 1,), (), (hops[1] - 1,), ())
    return pl.pallas_call(
        lambda *refs: project_kernel(hops, *refs),
        out_shape=[terms(*lead) for lead in leads],
        grid_spec=pltpu.PrefetchScalarGridSpec(
            num_scalar_prefetch=1,
            grid=(STEPS,),
            in_specs=[
                pl.BlockSpec((512, 512), lambda i, s: (0, 0)),
                pl.BlockSpec((512, 512), lambda i, s: (0, 0)),
                pl.BlockSpec((512, TILE), lambda i, s: (0, s[0] * (2 * STEPS) + chunk * STEPS + i)),
                pl.BlockSpec((256, TILE), lambda i, s: (0, i)),
                pl.BlockSpec((256, TILE), lambda i, s: (0, i)),
            ],
            out_specs=[block(*lead) for lead in leads],
            scratch_shapes=[pltpu.VMEM((512, TILE), BF)],
        ),
        cost_estimate=pl.CostEstimate(flops=2 * 512 * 1024 * HALF, bytes_accessed=7 << 20, transcendentals=0),
        name="project",
    )(place, a, b, w_out, wb, wc)


def layer(queries, keys, values, routes, gates, block_mask, w_out):
    ctx = lax.axis_index("ctx")
    head = lax.axis_index("head")
    x, j = ctx // NJ, ctx % NJ
    y, z = head // NZ, head % NZ

    def move_ctx(v, f):
        return lax.ppermute(v, "ctx", [(i, f(i)) for i in range(16)])

    def move_head(v, f):
        return lax.ppermute(v, "head", [(i, f(i)) for i in range(16)])

    def swap(i):
        return i ^ NZ

    w_fetched = []
    for n in range(2):
        given = lax.dynamic_slice(w_out, ((ctx % 2) * 256, (2 * (1 - y) + n) * HALF), (256, HALF))
        w_fetched.append(move_head(given, swap))

    kv = jnp.concatenate([keys, values.T], axis=0)
    kv2 = move_ctx(kv, lambda i: i ^ 2)
    kv1 = move_ctx(kv, lambda i: i ^ 1)

    head_ids = jnp.arange(H, dtype=jnp.int32)
    onehot = (routes[:, :, None] == head_ids[None, None, :]).astype(F32)
    per_token = jnp.sum(onehot, axis=1)
    below = (jnp.arange(32)[:, None] > jnp.arange(32)[None, :]).astype(F32)
    earlier = jnp.dot(below, per_token, preferred_element_type=F32)
    ranking = jnp.sum(onehot * earlier[:, None, :], axis=2).astype(jnp.int32)
    target = (routes * CAP + ranking).T.reshape(1, 512)
    gate_row = gates.T.reshape(1, 512)
    packed = pl.pallas_call(
        pack_kernel,
        out_shape=jax.ShapeDtypeStruct((16, 80, HD), BF),
        in_specs=[vmem()] * 3,
        out_specs=vmem(),
        compiler_params=grant(12),
        name="pack",
    )(queries, target, gate_row)
    arrived = lax.all_to_all(packed, "head", split_axis=0, concat_axis=0, tiled=True)
    q_own = arrived[:, :64, :]
    meta = arrived[:, 64:68, :64].astype(F32).reshape(16, 4, 4, CAP).transpose(1, 2, 0, 3).reshape(4, 4, 256)
    tok = meta[0] - 1.0
    gate = meta[1] + meta[2] + meta[3]
    dev = (jnp.arange(256) // CAP).astype(F32)
    in_block = jnp.maximum(tok, 0.0) + (dev[None, :] % 4.0) * 32.0

    a_id = jnp.arange(64)
    usable = (block_mask == 1) & (a_id[None, :] < a_id[:, None])
    usable = lax.dynamic_index_in_dim(usable.reshape(NX, NJ, 4, NX, NJ, 4), j, 1, keepdims=False)
    usable = lax.dynamic_index_in_dim(usable, x, 2, keepdims=False)
    usable = jnp.stack([lax.dynamic_index_in_dim(usable, j ^ i, 2, keepdims=False) for i in range(4)], axis=2)
    usable = jnp.stack([lax.dynamic_index_in_dim(usable, (x + dx) % NX, 0, keepdims=False) for dx in range(4)])
    flags = jnp.any(usable, axis=1).astype(jnp.int32).reshape(4, 16)
    bias = jnp.where(usable, 0.0, 2.0 * NEG).reshape(4, 4, 16).transpose(0, 2, 1)
    bias = jnp.concatenate([bias, jnp.full((4, 8, 4), 2.0 * NEG, F32)], axis=1)
    bias = jnp.repeat(bias, 64, axis=2).reshape(96, 256)
    same = (jnp.arange(256)[None, :] // 64) == jnp.arange(4)[:, None]
    earlier_ok = jnp.where(bias[0:4] == 0.0, 127.0, -1.0)
    lim = jnp.where(same[None], in_block[:, None, :], earlier_ok[None]).reshape(16, 256)

    q1 = move_ctx(q_own, lambda i: (i - 4) % 16)
    q2 = move_ctx(q_own, lambda i: (i - 8) % 16)
    q3 = move_ctx(q_own, lambda i: (i - 12) % 16)
    kv3 = move_ctx(kv2, lambda i: i ^ 1)
    kvs = (kv, kv1, kv2, kv3)
    parts = attend((1, 2, 3), flags, bias, lim, (q1, q2, q3), kvs)
    back = [move_ctx(part, lambda i: (i + 4 * dx) % 16) for dx, part in ((1, parts[0]), (2, parts[1]), (3, parts[2]))]
    (own,) = attend((0,), flags, bias, lim, (q_own,), kvs)
    sent = pl.pallas_call(
        merge_kernel,
        out_shape=jax.ShapeDtypeStruct((528, 256), BF),
        in_specs=[vmem()] * 6,
        out_specs=vmem(),
        compiler_params=grant(8),
        name="merge",
    )(own, *back, tok, gate)
    got = move_head(sent, swap)
    w_swapped = []
    for n in range(2):
        w_swapped.append(move_ctx(w_fetched[n], lambda i: i ^ 1))
    tokens = jax.ShapeDtypeStruct((512, 512), BF)
    mine = pl.pallas_call(
        place_kernel, out_shape=tokens, in_specs=[vmem()], out_specs=vmem(), compiler_params=grant(8), name="place"
    )(sent)
    theirs = pl.pallas_call(
        spread_kernel,
        out_shape=tokens,
        in_specs=[pl.BlockSpec(memory_space=pltpu.SMEM), vmem()],
        out_specs=vmem(),
        compiler_params=grant(8),
        name="spread",
    )((ctx % 2).reshape(1), got)

    def shift(step):
        return lambda i: (i // NZ) * NZ + (i % NZ + step) % NZ

    here, there = [], []
    for chunk, hops in ((0, (4, 3)), (1, (3, 4))):
        up0, up, down0, down, total = project(
            jnp.stack([y, z]), chunk, hops, mine, theirs, w_out, w_fetched[chunk], w_swapped[chunk]
        )
        total = total.astype(F32)
        for step, length, message, rest in ((1, hops[0], up0, up), (-1, hops[1], down0, down)):
            for hop in range(length):
                if hop:
                    message = (message.astype(F32) + rest[hop - 1].astype(F32)).astype(BF)
                message = move_head(message, shift(step))
            total = total + message.astype(F32)
        total = total.astype(BF)
        here.append(lax.dynamic_index_in_dim(total, y, 0, keepdims=False))
        there.append(move_head(lax.dynamic_index_in_dim(total, 1 - y, 0, keepdims=False), swap))
    low = [jnp.where(y == 0, h, t) for h, t in zip(here, there)]
    high = [jnp.where(y == 0, t, h) for h, t in zip(here, there)]
    return jnp.concatenate(low + high, axis=1)


def solution(mesh):
    placed = (
        P(("ctx", "head"), None),
        P("ctx", "head"),
        P("ctx", "head"),
        P(("ctx", "head"), None),
        P(("ctx", "head"), None),
        P(),
        P("head", None),
    )
    return jax.shard_map(layer, mesh=mesh, in_specs=placed, out_specs=P(("ctx", "head"), None), check_vma=False)
```

profile of v0, /device:TPU:4, one launch (start us, length us, event | category | flops | bytes accessed | tf_op | source)
XLA Modules:
  0.0 186.6 jit_solution(5183186199932201443)
XLA Ops:
  2.4 1.7 collective-permute-start.1
  6.4 10.9 %all-to-all-start = ((bf16[16,80,128]{2,1,0:T(8,128)(2,1)}), bf16[16,80,128]{2,1,0:T(8,128)(2,1)}, u32[]{:S(2)}, u32[]{:S(2)}) async-start(bf16[16,80,128]{2,1,0:T(8,128)(2,1)} %pack.1), calls=%async_computation | async-start | bytes 655360 | tf_op jit(solution)/shard_map/all_to_all | solution.py:326
  17.4 3.1 %fusion.17 = (bf16[256,2048]{1,0:T(8,128)(2,1)}, bf16[256,2048]{1,0:T(8,128)(2,1)}) fusion(bf16[512,8192]{1,0:T(8,128)(2,1)} %refs_3_.3, s32[]{:T(128)S(6)} %select_n.199, s32[]{:T(128)S(6)} %select_n.200, s32[]{:T(128)S(6)} %select_n.204), kind=kLoop, calls=%fused_computation.76 | loop fusion | bytes 4194316 | tf_op jit(solution)/shard_map/dynamic_slice | solution.py:303
  20.5 3.3 %collective-permute-start.10 = (bf16[256,2048]{1,0:T(8,128)(2,1)}, bf16[256,2048]{1,0:T(8,128)(2,1)}, u32[]{:S(2)}, u32[]{:S(2)}) collective-permute-start(bf16[256,2048]{1,0:T(8,128)(2,1)} %get-tuple-element.31), channel_id=1, source_target_pairs={{0,128},{16,144},{32,160},{48,176},{64,192},{80,208},{96,224},{112... | collective-permute-start | bytes 3145736 | tf_op jit(solution)/shard_map/ppermute | solution.py:296
  25.5 9.1 %all-to-all-done = bf16[16,80,128]{2,1,0:T(8,128)(2,1)} async-done(((bf16[16,80,128]{2,1,0:T(8,128)(2,1)}), bf16[16,80,128]{2,1,0:T(8,128)(2,1)}, u32[]{:S(2)}, u32[]{:S(2)}) %all-to-all-start) | async-done | bytes 327712 | tf_op jit(solution)/shard_map/all_to_all | solution.py:326
  36.9 5.2 %collective-permute-done.3.refs_3_ = bf16[16,64,128]{2,1,0:T(8,128)(2,1)} collective-permute-done((bf16[16,64,128]{2,1,0:T(8,128)(2,1)S(1)}, bf16[16,64,128]{2,1,0:T(8,128)(2,1)}, u32[]{:S(2)}, u32[]{:S(2)}) %collective-permute-start.3) | collective-permute-done | bytes 262176 | tf_op jit(solution)/shard_map/ppermute | solution.py:293
  46.0 5.5 %collective-permute-done.4.refs_4_ = bf16[16,64,128]{2,1,0:T(8,128)(2,1)} collective-permute-done((bf16[16,64,128]{2,1,0:T(8,128)(2,1)S(1)}, bf16[16,64,128]{2,1,0:T(8,128)(2,1)}, u32[]{:S(2)}, u32[]{:S(2)}) %collective-permute-start.4) | collective-permute-done | bytes 262176 | tf_op jit(solution)/shard_map/ppermute | solution.py:293
  53.2 3.9 %collective-permute-done.10.refs_4_ = bf16[256,2048]{1,0:T(8,128)(2,1)} collective-permute-done((bf16[256,2048]{1,0:T(8,128)(2,1)}, bf16[256,2048]{1,0:T(8,128)(2,1)}, u32[]{:S(2)}, u32[]{:S(2)}) %collective-permute-start.10) | collective-permute-done | bytes 1048608 | tf_op jit(solution)/shard_map/ppermute | solution.py:296
  57.1 21.3 %collective-permute-done.20.refs_4_ = bf16[256,2048]{1,0:T(8,128)(2,1)} collective-permute-done((bf16[256,2048]{1,0:T(8,128)(2,1)}, bf16[256,2048]{1,0:T(8,128)(2,1)}, u32[]{:S(2)}, u32[]{:S(2)}) %collective-permute-start.20) | collective-permute-done | bytes 1048608 | tf_op jit(solution)/shard_map/ppermute | solution.py:296
  78.4 6.2 %attend.3 = (bf16[528,256]{1,0:T(8,128)(2,1)}, bf16[528,256]{1,0:T(8,128)(2,1)}, bf16[528,256]{1,0:T(8,128)(2,1)}) custom-call(s32[4,16]{1,0:T(4,128)S(1)} %reshape.178.refs_0_, f32[96,256]{1,0:T(8,128)S(1)} %reshape_reshape.3.refs_1_, f32[16,256]{1,0:T(8,128)S(1)} %select_n.197.refs_2_, bf16[16,64,128]{2,1,0:T(8,128)(2,1)} %collective-permute-done.3.refs_3_, ...), custom_call_target="tpu_custom_call" | custom-call | flops 3221225472 | bytes 5242880 | tf_op jit(solution)/shard_map/attend/pallas_call | solution.py:157
  84.7 8.7 %collective-permute-start.7 = (bf16[528,256]{1,0:T(8,128)(2,1)}, bf16[528,256]{1,0:T(8,128)(2,1)}, u32[]{:S(2)}, u32[]{:S(2)}) collective-permute-start(bf16[528,256]{1,0:T(8,128)(2,1)} %get-tuple-element.19), channel_id=1, source_target_pairs={{0,8},{1,9},{2,10},{3,11},{4,12},{5,13},{6,14},{7,15},{8,0},{9,1},... | collective-permute-start | bytes 811016 | tf_op jit(solution)/shard_map/ppermute | solution.py:293
  93.4 2.3 %collective-permute-start.8 = (bf16[528,256]{1,0:T(8,128)(2,1)}, bf16[528,256]{1,0:T(8,128)(2,1)}, u32[]{:S(2)}, u32[]{:S(2)}) collective-permute-start(bf16[528,256]{1,0:T(8,128)(2,1)} %get-tuple-element.20), channel_id=1, source_target_pairs={{0,12},{1,13},{2,14},{3,15},{4,0},{5,1},{6,2},{7,3},{8,4},{9,5},{1... | collective-permute-start | bytes 811016 | tf_op jit(solution)/shard_map/ppermute | solution.py:293
  96.6 2.4 %attend.2.a_ref = bf16[528,256]{1,0:T(8,128)(2,1)S(1)} custom-call(s32[4,16]{1,0:T(4,128)S(1)} %reshape.178.refs_0_, f32[96,256]{1,0:T(8,128)S(1)} %reshape_reshape.3.refs_1_, f32[16,256]{1,0:T(8,128)S(1)} %select_n.197.refs_2_, bf16[16,64,128]{2,1,0:T(8,128)(2,1)S(1)} %slice.75.refs_3_, bf16[1024,512]{1,0:T(8,128)(2,1)S(1)} %pad_maximum_fusion.refs_4_.refs_6_, ...), custom_call_target="tpu_custom_call" | custom-call | flops 1073741824 | bytes 5242880 | tf_op jit(solution)/shard_map/attend/pallas_call | solution.py:157
  99.0 6.3 %collective-permute-done.7.c_ref = bf16[528,256]{1,0:T(8,128)(2,1)} collective-permute-done((bf16[528,256]{1,0:T(8,128)(2,1)}, bf16[528,256]{1,0:T(8,128)(2,1)}, u32[]{:S(2)}, u32[]{:S(2)}) %collective-permute-start.7) | collective-permute-done | bytes 270368 | tf_op jit(solution)/shard_map/ppermute | solution.py:293
  110.7 8.3 %collective-permute-done.9.got_ref = bf16[528,256]{1,0:T(8,128)(2,1)S(1)} collective-permute-done((bf16[528,256]{1,0:T(8,128)(2,1)S(1)}, bf16[528,256]{1,0:T(8,128)(2,1)S(1)}, u32[]{:S(2)}, u32[]{:S(2)}) %collective-permute-start.9) | collective-permute-done | bytes 270368 | tf_op jit(solution)/shard_map/ppermute | solution.py:296
  120.1 6.8 %project.2 = (bf16[2,32,2048]{2,1,0:T(8,128)(2,1)}, bf16[3,2,32,2048]{3,2,1,0:T(8,128)(2,1)}, bf16[2,32,2048]{2,1,0:T(8,128)(2,1)}, bf16[2,2,32,2048]{3,2,1,0:T(8,128)(2,1)}, bf16[2,32,2048]{2,1,0:T(8,128)(2,1)}) custom-call(s32[2]{0:T(128)} %pad_add_fusion.1.refs_0_, bf16[512,512]{1,0:T(8,128)(2,1)} %copy-done, bf16[512,512]{1,0:T(8,128)(2,1)} %copy-done.1, ...), custom_call_target="tpu_custom_call" | custom-call | flops 2147483648 | bytes 7340032 | tf_op jit(solution)/shard_map/project/pallas_call | solution.py:265
  126.9 2.0 %collective-permute-start.12 = (bf16[2,32,2048]{2,1,0:T(8,128)(2,1)}, bf16[2,32,2048]{2,1,0:T(8,128)(2,1)S(1)}, u32[]{:S(2)}, u32[]{:S(2)}) collective-permute-start(bf16[2,32,2048]{2,1,0:T(8,128)(2,1)} %get-tuple-element.22), channel_id=1, source_target_pairs={{0,16},{16,32},{32,48},{48,64},{64,80},{80,96},{96,112},{112,0},{1... | collective-permute-start | bytes 786440 | tf_op jit(solution)/shard_map/ppermute | solution.py:296
  128.9 4.1 %collective-permute-start.16 = (bf16[2,32,2048]{2,1,0:T(8,128)(2,1)}, bf16[2,32,2048]{2,1,0:T(8,128)(2,1)S(1)}, u32[]{:S(2)}, u32[]{:S(2)}) collective-permute-start(bf16[2,32,2048]{2,1,0:T(8,128)(2,1)} %get-tuple-element.24), channel_id=1, source_target_pairs={{0,112},{16,0},{32,16},{48,32},{64,48},{80,64},{96,80},{112,96},{1... | collective-permute-start | bytes 786440 | tf_op jit(solution)/shard_map/ppermute | solution.py:296
  133.0 6.8 %project.3 = (bf16[2,32,2048]{2,1,0:T(8,128)(2,1)}, bf16[2,2,32,2048]{3,2,1,0:T(8,128)(2,1)}, bf16[2,32,2048]{2,1,0:T(8,128)(2,1)}, bf16[3,2,32,2048]{3,2,1,0:T(8,128)(2,1)}, bf16[2,32,2048]{2,1,0:T(8,128)(2,1)}) custom-call(s32[2]{0:T(128)} %pad_add_fusion.1.refs_0_, bf16[512,512]{1,0:T(8,128)(2,1)} %copy-done, bf16[512,512]{1,0:T(8,128)(2,1)} %copy-done.1, ...), custom_call_target="tpu_custom_call" | custom-call | flops 2147483648 | bytes 7340032 | tf_op jit(solution)/shard_map/project/pallas_call | solution.py:265
  139.9 3.2 %collective-permute-start.25 = (bf16[2,32,2048]{2,1,0:T(8,128)(2,1)}, bf16[2,32,2048]{2,1,0:T(8,128)(2,1)S(1)}, u32[]{:S(2)}, u32[]{:S(2)}) collective-permute-start(bf16[2,32,2048]{2,1,0:T(8,128)(2,1)} %get-tuple-element.29), channel_id=1, source_target_pairs={{0,112},{16,0},{32,16},{48,32},{64,48},{80,64},{96,80},{112,96},{1... | collective-permute-start | bytes 786440 | tf_op jit(solution)/shard_map/ppermute | solution.py:296
  143.4 3.3 %collective-permute-start.17 = (bf16[2,32,2048]{2,1,0:T(8,128)(2,1)S(1)}, bf16[2,32,2048]{2,1,0:T(8,128)(2,1)S(1)}, u32[]{:S(2)}, u32[]{:S(2)}) collective-permute-start(bf16[2,32,2048]{2,1,0:T(8,128)(2,1)S(1)} %fusion.6), channel_id=1, source_target_pairs={{0,112},{16,0},{32,16},{48,32},{64,48},{80,64},{96,80},{112,96},{1... | collective-permute-start | bytes 786440 | tf_op jit(solution)/shard_map/ppermute | solution.py:296
  146.7 3.8 %collective-permute-done.22 = bf16[2,32,2048]{2,1,0:T(8,128)(2,1)S(1)} collective-permute-done((bf16[2,32,2048]{2,1,0:T(8,128)(2,1)}, bf16[2,32,2048]{2,1,0:T(8,128)(2,1)S(1)}, u32[]{:S(2)}, u32[]{:S(2)}) %collective-permute-start.22) | collective-permute-done | bytes 262176 | tf_op jit(solution)/shard_map/ppermute | solution.py:296
  151.7 3.3 %collective-permute-start.26 = (bf16[2,32,2048]{2,1,0:T(8,128)(2,1)S(1)}, bf16[2,32,2048]{2,1,0:T(8,128)(2,1)S(1)}, u32[]{:S(2)}, u32[]{:S(2)}) collective-permute-start(bf16[2,32,2048]{2,1,0:T(8,128)(2,1)S(1)} %fusion.2), channel_id=1, source_target_pairs={{0,112},{16,0},{32,16},{48,32},{64,48},{80,64},{96,80},{112,96},{1... | collective-permute-start | bytes 786440 | tf_op jit(solution)/shard_map/ppermute | solution.py:296
  156.3 3.5 %collective-permute-start.18 = (bf16[2,32,2048]{2,1,0:T(8,128)(2,1)S(1)}, bf16[2,32,2048]{2,1,0:T(8,128)(2,1)S(1)}, u32[]{:S(2)}, u32[]{:S(2)}) collective-permute-start(bf16[2,32,2048]{2,1,0:T(8,128)(2,1)S(1)} %fusion.5), channel_id=1, source_target_pairs={{0,112},{16,0},{32,16},{48,32},{64,48},{80,64},{96,80},{112,96},{1... | collective-permute-start | bytes 786440 | tf_op jit(solution)/shard_map/ppermute | solution.py:296
  159.9 2.1 %collective-permute-done.23 = bf16[2,32,2048]{2,1,0:T(8,128)(2,1)S(1)} collective-permute-done((bf16[2,32,2048]{2,1,0:T(8,128)(2,1)S(1)}, bf16[2,32,2048]{2,1,0:T(8,128)(2,1)S(1)}, u32[]{:S(2)}, u32[]{:S(2)}) %collective-permute-start.23) | collective-permute-done | bytes 262176 | tf_op jit(solution)/shard_map/ppermute | solution.py:296
  162.2 3.3 %collective-permute-start.27 = (bf16[2,32,2048]{2,1,0:T(8,128)(2,1)S(1)}, bf16[2,32,2048]{2,1,0:T(8,128)(2,1)S(1)}, u32[]{:S(2)}, u32[]{:S(2)}) collective-permute-start(bf16[2,32,2048]{2,1,0:T(8,128)(2,1)S(1)} %fusion.1), channel_id=1, source_target_pairs={{0,112},{16,0},{32,16},{48,32},{64,48},{80,64},{96,80},{112,96},{1... | collective-permute-start | bytes 786440 | tf_op jit(solution)/shard_map/ppermute | solution.py:296
  165.5 2.1 %collective-permute-done.14 = bf16[2,32,2048]{2,1,0:T(8,128)(2,1)S(1)} collective-permute-done((bf16[2,32,2048]{2,1,0:T(8,128)(2,1)S(1)}, bf16[2,32,2048]{2,1,0:T(8,128)(2,1)S(1)}, u32[]{:S(2)}, u32[]{:S(2)}) %collective-permute-start.14) | collective-permute-done | bytes 262176 | tf_op jit(solution)/shard_map/ppermute | solution.py:296
  167.7 3.2 %collective-permute-done.27 = bf16[2,32,2048]{2,1,0:T(8,128)(2,1)S(1)} collective-permute-done((bf16[2,32,2048]{2,1,0:T(8,128)(2,1)S(1)}, bf16[2,32,2048]{2,1,0:T(8,128)(2,1)S(1)}, u32[]{:S(2)}, u32[]{:S(2)}) %collective-permute-start.27) | collective-permute-done | bytes 262176 | tf_op jit(solution)/shard_map/ppermute | solution.py:296
  171.0 3.8 %collective-permute-start.28 = (bf16[2,32,2048]{2,1,0:T(8,128)(2,1)S(1)}, bf16[2,32,2048]{2,1,0:T(8,128)(2,1)S(1)}, u32[]{:S(2)}, u32[]{:S(2)}) collective-permute-start(bf16[2,32,2048]{2,1,0:T(8,128)(2,1)S(1)} %fusion), channel_id=1, source_target_pairs={{0,112},{16,0},{32,16},{48,32},{64,48},{80,64},{96,80},{112,96},{1... | collective-permute-start | bytes 786440 | tf_op jit(solution)/shard_map/ppermute | solution.py:296
  174.7 2.5 %collective-permute-done.15 = bf16[2,32,2048]{2,1,0:T(8,128)(2,1)S(1)} collective-permute-done((bf16[2,32,2048]{2,1,0:T(8,128)(2,1)S(1)}, bf16[2,32,2048]{2,1,0:T(8,128)(2,1)S(1)}, u32[]{:S(2)}, u32[]{:S(2)}) %collective-permute-start.15) | collective-permute-done | bytes 262176 | tf_op jit(solution)/shard_map/ppermute | solution.py:296
  178.7 2.5 %collective-permute-start.29 = (bf16[32,2048]{1,0:T(8,128)(2,1)S(1)}, bf16[32,2048]{1,0:T(8,128)(2,1)S(1)}, u32[]{:S(2)}, u32[]{:S(2)}) collective-permute-start(bf16[32,2048]{1,0:T(8,128)(2,1)S(1)} %dynamic-slice_bitcast_fusion), channel_id=1, source_target_pairs={{0,128},{16,144},{32,160},{48,176},{64,192},{80,208},{96,224},{112... | collective-permute-start | bytes 393224 | tf_op jit(solution)/shard_map/ppermute | solution.py:296
  181.2 3.1 %collective-permute-done.19 = bf16[32,2048]{1,0:T(8,128)(2,1)S(1)} collective-permute-done((bf16[32,2048]{1,0:T(8,128)(2,1)S(1)}, bf16[32,2048]{1,0:T(8,128)(2,1)S(1)}, u32[]{:S(2)}, u32[]{:S(2)}) %collective-permute-start.19) | collective-permute-done | bytes 131104 | tf_op jit(solution)/shard_map/ppermute | solution.py:296
  (129 shorter events, 28.3 us)
Async XLA Ops:
  2.4 33.8 %collective-permute-start.1 = (bf16[1024,512]{1,0:T(8,128)(2,1)S(1)}, bf16[1024,512]{1,0:T(8,128)(2,1)S(1)}, u32[]{:S(2)}, u32[]{:S(2)}) collective-permute-start(bf16[1024,512]{1,0:T(8,128)(2,1)S(1)} %pad_maximum_fusion.refs_4_.refs_6_), channel_id=1, source_target_pairs={{0,2},{1,3},{2,0},{3,1},{4,6},{5,7},{6,4},{7,5},{8,10},{9,11},{10,... | collective-permute-start | bytes 3145736 | tf_op jit(solution)/shard_map/ppermute | solution.py:293
  4.1 74.3 %collective-permute-start = (bf16[1024,512]{1,0:T(8,128)(2,1)S(1)}, bf16[1024,512]{1,0:T(8,128)(2,1)S(1)}, u32[]{:S(2)}, u32[]{:S(2)}) collective-permute-start(bf16[1024,512]{1,0:T(8,128)(2,1)S(1)} %pad_maximum_fusion.refs_4_.refs_6_), channel_id=1, source_target_pairs={{0,1},{1,0},{2,3},{3,2},{4,5},{5,4},{6,7},{7,6},{8,9},{9,8},{10,11... | collective-permute-start | bytes 3145736 | tf_op jit(solution)/shard_map/ppermute | solution.py:293
  6.4 28.2 %all-to-all-start = ((bf16[16,80,128]{2,1,0:T(8,128)(2,1)}), bf16[16,80,128]{2,1,0:T(8,128)(2,1)}, u32[]{:S(2)}, u32[]{:S(2)}) async-start(bf16[16,80,128]{2,1,0:T(8,128)(2,1)} %pack.1), calls=%async_computation | async-start | bytes 655360 | tf_op jit(solution)/shard_map/all_to_all | solution.py:326
  20.5 36.6 %collective-permute-start.10 = (bf16[256,2048]{1,0:T(8,128)(2,1)}, bf16[256,2048]{1,0:T(8,128)(2,1)}, u32[]{:S(2)}, u32[]{:S(2)}) collective-permute-start(bf16[256,2048]{1,0:T(8,128)(2,1)} %get-tuple-element.31), channel_id=1, source_target_pairs={{0,128},{16,144},{32,160},{48,176},{64,192},{80,208},{96,224},{112... | collective-permute-start | bytes 3145736 | tf_op jit(solution)/shard_map/ppermute | solution.py:296
  23.8 54.6 %collective-permute-start.20 = (bf16[256,2048]{1,0:T(8,128)(2,1)}, bf16[256,2048]{1,0:T(8,128)(2,1)}, u32[]{:S(2)}, u32[]{:S(2)}) collective-permute-start(bf16[256,2048]{1,0:T(8,128)(2,1)} %get-tuple-element.32), channel_id=1, source_target_pairs={{0,128},{16,144},{32,160},{48,176},{64,192},{80,208},{96,224},{112... | collective-permute-start | bytes 3145736 | tf_op jit(solution)/shard_map/ppermute | solution.py:296
  35.6 6.6 %collective-permute-start.3 = (bf16[16,64,128]{2,1,0:T(8,128)(2,1)S(1)}, bf16[16,64,128]{2,1,0:T(8,128)(2,1)}, u32[]{:S(2)}, u32[]{:S(2)}) collective-permute-start(bf16[16,64,128]{2,1,0:T(8,128)(2,1)S(1)} %slice.75.refs_3_), channel_id=1, source_target_pairs={{0,12},{1,13},{2,14},{3,15},{4,0},{5,1},{6,2},{7,3},{8,4},{9,5},{1... | collective-permute-start | bytes 786440 | tf_op jit(solution)/shard_map/ppermute | solution.py:293
  36.2 42.2 %collective-permute-start.2 = (bf16[1024,512]{1,0:T(8,128)(2,1)S(1)}, bf16[1024,512]{1,0:T(8,128)(2,1)}, u32[]{:S(2)}, u32[]{:S(2)}) collective-permute-start(bf16[1024,512]{1,0:T(8,128)(2,1)S(1)} %collective-permute-done.1.refs_6_.refs_8_), channel_id=1, source_target_pairs={{0,1},{1,0},{2,3},{3,2},{4,5},{5,4},{6,7},{7,6},{8,9},{9,8},{10,11... | collective-permute-start | bytes 3145736 | tf_op jit(solution)/shard_map/ppermute | solution.py:293
  42.1 9.4 %collective-permute-start.4 = (bf16[16,64,128]{2,1,0:T(8,128)(2,1)S(1)}, bf16[16,64,128]{2,1,0:T(8,128)(2,1)}, u32[]{:S(2)}, u32[]{:S(2)}) collective-permute-start(bf16[16,64,128]{2,1,0:T(8,128)(2,1)S(1)} %slice.75.refs_3_), channel_id=1, source_target_pairs={{0,8},{1,9},{2,10},{3,11},{4,12},{5,13},{6,14},{7,15},{8,0},{9,1},... | collective-permute-start | bytes 786440 | tf_op jit(solution)/shard_map/ppermute | solution.py:293
  51.5 26.9 %collective-permute-start.5 = (bf16[16,64,128]{2,1,0:T(8,128)(2,1)S(1)}, bf16[16,64,128]{2,1,0:T(8,128)(2,1)}, u32[]{:S(2)}, u32[]{:S(2)}) collective-permute-start(bf16[16,64,128]{2,1,0:T(8,128)(2,1)S(1)} %slice.75.refs_3_), channel_id=1, source_target_pairs={{0,4},{1,5},{2,6},{3,7},{4,8},{5,9},{6,10},{7,11},{8,12},{9,13},{1... | collective-permute-start | bytes 786440 | tf_op jit(solution)/shard_map/ppermute | solution.py:293
  57.1 63.0 %collective-permute-start.11 = (bf16[256,2048]{1,0:T(8,128)(2,1)}, bf16[256,2048]{1,0:T(8,128)(2,1)}, u32[]{:S(2)}, u32[]{:S(2)}) collective-permute-start(bf16[256,2048]{1,0:T(8,128)(2,1)} %collective-permute-done.10.refs_4_), channel_id=1, source_target_pairs={{0,1},{1,0},{2,3},{3,2},{4,5},{5,4},{6,7},{7,6},{8,9},{9,8},{10,11... | collective-permute-start | bytes 3145736 | tf_op jit(solution)/shard_map/ppermute | solution.py:293
  78.4 54.5 %collective-permute-start.21 = (bf16[256,2048]{1,0:T(8,128)(2,1)}, bf16[256,2048]{1,0:T(8,128)(2,1)}, u32[]{:S(2)}, u32[]{:S(2)}) collective-permute-start(bf16[256,2048]{1,0:T(8,128)(2,1)} %collective-permute-done.20.refs_4_), channel_id=1, source_target_pairs={{0,1},{1,0},{2,3},{3,2},{4,5},{5,4},{6,7},{7,6},{8,9},{9,8},{10,11... | collective-permute-start | bytes 3145736 | tf_op jit(solution)/shard_map/ppermute | solution.py:293
  84.6 14.4 %collective-permute-start.6 = (bf16[528,256]{1,0:T(8,128)(2,1)}, bf16[528,256]{1,0:T(8,128)(2,1)}, u32[]{:S(2)}, u32[]{:S(2)}) collective-permute-start(bf16[528,256]{1,0:T(8,128)(2,1)} %get-tuple-element.18), channel_id=1, source_target_pairs={{0,4},{1,5},{2,6},{3,7},{4,8},{5,9},{6,10},{7,11},{8,12},{9,13},{1... | collective-permute-start | bytes 811016 | tf_op jit(solution)/shard_map/ppermute | solution.py:293
  84.7 20.6 %collective-permute-start.7 = (bf16[528,256]{1,0:T(8,128)(2,1)}, bf16[528,256]{1,0:T(8,128)(2,1)}, u32[]{:S(2)}, u32[]{:S(2)}) collective-permute-start(bf16[528,256]{1,0:T(8,128)(2,1)} %get-tuple-element.19), channel_id=1, source_target_pairs={{0,8},{1,9},{2,10},{3,11},{4,12},{5,13},{6,14},{7,15},{8,0},{9,1},... | collective-permute-start | bytes 811016 | tf_op jit(solution)/shard_map/ppermute | solution.py:293
  93.4 13.4 %collective-permute-start.8 = (bf16[528,256]{1,0:T(8,128)(2,1)}, bf16[528,256]{1,0:T(8,128)(2,1)}, u32[]{:S(2)}, u32[]{:S(2)}) collective-permute-start(bf16[528,256]{1,0:T(8,128)(2,1)} %get-tuple-element.20), channel_id=1, source_target_pairs={{0,12},{1,13},{2,14},{3,15},{4,0},{5,1},{6,2},{7,3},{8,4},{9,5},{1... | collective-permute-start | bytes 811016 | tf_op jit(solution)/shard_map/ppermute | solution.py:293
  108.2 10.8 %collective-permute-start.9 = (bf16[528,256]{1,0:T(8,128)(2,1)S(1)}, bf16[528,256]{1,0:T(8,128)(2,1)S(1)}, u32[]{:S(2)}, u32[]{:S(2)}) collective-permute-start(bf16[528,256]{1,0:T(8,128)(2,1)S(1)} %merge.1.sent_ref), channel_id=1, source_target_pairs={{0,128},{16,144},{32,160},{48,176},{64,192},{80,208},{96,224},{112... | collective-permute-start | bytes 811016 | tf_op jit(solution)/shard_map/ppermute | solution.py:296
  126.9 16.2 %collective-permute-start.12 = (bf16[2,32,2048]{2,1,0:T(8,128)(2,1)}, bf16[2,32,2048]{2,1,0:T(8,128)(2,1)S(1)}, u32[]{:S(2)}, u32[]{:S(2)}) collective-permute-start(bf16[2,32,2048]{2,1,0:T(8,128)(2,1)} %get-tuple-element.22), channel_id=1, source_target_pairs={{0,16},{16,32},{32,48},{48,64},{64,80},{80,96},{96,112},{112,0},{1... | collective-permute-start | bytes 786440 | tf_op jit(solution)/shard_map/ppermute | solution.py:296
  128.9 14.4 %collective-permute-start.16 = (bf16[2,32,2048]{2,1,0:T(8,128)(2,1)}, bf16[2,32,2048]{2,1,0:T(8,128)(2,1)S(1)}, u32[]{:S(2)}, u32[]{:S(2)}) collective-permute-start(bf16[2,32,2048]{2,1,0:T(8,128)(2,1)} %get-tuple-element.24), channel_id=1, source_target_pairs={{0,112},{16,0},{32,16},{48,32},{64,48},{80,64},{96,80},{112,96},{1... | collective-permute-start | bytes 786440 | tf_op jit(solution)/shard_map/ppermute | solution.py:296
  139.8 10.7 %collective-permute-start.22 = (bf16[2,32,2048]{2,1,0:T(8,128)(2,1)}, bf16[2,32,2048]{2,1,0:T(8,128)(2,1)S(1)}, u32[]{:S(2)}, u32[]{:S(2)}) collective-permute-start(bf16[2,32,2048]{2,1,0:T(8,128)(2,1)} %get-tuple-element.27), channel_id=1, source_target_pairs={{0,16},{16,32},{32,48},{48,64},{64,80},{80,96},{96,112},{112,0},{1... | collective-permute-start | bytes 786440 | tf_op jit(solution)/shard_map/ppermute | solution.py:296
  139.9 11.7 %collective-permute-start.25 = (bf16[2,32,2048]{2,1,0:T(8,128)(2,1)}, bf16[2,32,2048]{2,1,0:T(8,128)(2,1)S(1)}, u32[]{:S(2)}, u32[]{:S(2)}) collective-permute-start(bf16[2,32,2048]{2,1,0:T(8,128)(2,1)} %get-tuple-element.29), channel_id=1, source_target_pairs={{0,112},{16,0},{32,16},{48,32},{64,48},{80,64},{96,80},{112,96},{1... | collective-permute-start | bytes 786440 | tf_op jit(solution)/shard_map/ppermute | solution.py:296
  143.2 12.9 %collective-permute-start.13 = (bf16[2,32,2048]{2,1,0:T(8,128)(2,1)S(1)}, bf16[2,32,2048]{2,1,0:T(8,128)(2,1)S(1)}, u32[]{:S(2)}, u32[]{:S(2)}) collective-permute-start(bf16[2,32,2048]{2,1,0:T(8,128)(2,1)S(1)} %fusion.9), channel_id=1, source_target_pairs={{0,16},{16,32},{32,48},{48,64},{64,80},{80,96},{96,112},{112,0},{1... | collective-permute-start | bytes 786440 | tf_op jit(solution)/shard_map/ppermute | solution.py:296
  143.4 12.9 %collective-permute-start.17 = (bf16[2,32,2048]{2,1,0:T(8,128)(2,1)S(1)}, bf16[2,32,2048]{2,1,0:T(8,128)(2,1)S(1)}, u32[]{:S(2)}, u32[]{:S(2)}) collective-permute-start(bf16[2,32,2048]{2,1,0:T(8,128)(2,1)S(1)} %fusion.6), channel_id=1, source_target_pairs={{0,112},{16,0},{32,16},{48,32},{64,48},{80,64},{96,80},{112,96},{1... | collective-permute-start | bytes 786440 | tf_op jit(solution)/shard_map/ppermute | solution.py:296
  151.5 10.5 %collective-permute-start.23 = (bf16[2,32,2048]{2,1,0:T(8,128)(2,1)S(1)}, bf16[2,32,2048]{2,1,0:T(8,128)(2,1)S(1)}, u32[]{:S(2)}, u32[]{:S(2)}) collective-permute-start(bf16[2,32,2048]{2,1,0:T(8,128)(2,1)S(1)} %fusion.4), channel_id=1, source_target_pairs={{0,16},{16,32},{32,48},{48,64},{64,80},{80,96},{96,112},{112,0},{1... | collective-permute-start | bytes 786440 | tf_op jit(solution)/shard_map/ppermute | solution.py:296
  151.7 10.5 %collective-permute-start.26 = (bf16[2,32,2048]{2,1,0:T(8,128)(2,1)S(1)}, bf16[2,32,2048]{2,1,0:T(8,128)(2,1)S(1)}, u32[]{:S(2)}, u32[]{:S(2)}) collective-permute-start(bf16[2,32,2048]{2,1,0:T(8,128)(2,1)S(1)} %fusion.2), channel_id=1, source_target_pairs={{0,112},{16,0},{32,16},{48,32},{64,48},{80,64},{96,80},{112,96},{1... | collective-permute-start | bytes 786440 | tf_op jit(solution)/shard_map/ppermute | solution.py:296
  156.2 11.4 %collective-permute-start.14 = (bf16[2,32,2048]{2,1,0:T(8,128)(2,1)S(1)}, bf16[2,32,2048]{2,1,0:T(8,128)(2,1)S(1)}, u32[]{:S(2)}, u32[]{:S(2)}) collective-permute-start(bf16[2,32,2048]{2,1,0:T(8,128)(2,1)S(1)} %fusion.8), channel_id=1, source_target_pairs={{0,16},{16,32},{32,48},{48,64},{64,80},{80,96},{96,112},{112,0},{1... | collective-permute-start | bytes 786440 | tf_op jit(solution)/shard_map/ppermute | solution.py:296
  156.3 22.3 %copy-start.8 = (bf16[2,32,2048]{2,1,0:T(8,128)(2,1)S(1)}, bf16[2,32,2048]{2,1,0:T(8,128)(2,1)}, u32[]{:S(2)}) copy-start(bf16[2,32,2048]{2,1,0:T(8,128)(2,1)} %get-tuple-element.26) | copy-start | bytes 786436
  156.3 18.4 %collective-permute-start.18 = (bf16[2,32,2048]{2,1,0:T(8,128)(2,1)S(1)}, bf16[2,32,2048]{2,1,0:T(8,128)(2,1)S(1)}, u32[]{:S(2)}, u32[]{:S(2)}) collective-permute-start(bf16[2,32,2048]{2,1,0:T(8,128)(2,1)S(1)} %fusion.5), channel_id=1, source_target_pairs={{0,112},{16,0},{32,16},{48,32},{64,48},{80,64},{96,80},{112,96},{1... | collective-permute-start | bytes 786440 | tf_op jit(solution)/shard_map/ppermute | solution.py:296
  162.0 16.0 %collective-permute-start.24 = (bf16[2,32,2048]{2,1,0:T(8,128)(2,1)S(1)}, bf16[2,32,2048]{2,1,0:T(8,128)(2,1)S(1)}, u32[]{:S(2)}, u32[]{:S(2)}) collective-permute-start(bf16[2,32,2048]{2,1,0:T(8,128)(2,1)S(1)} %fusion.3), channel_id=1, source_target_pairs={{0,16},{16,32},{32,48},{48,64},{64,80},{80,96},{96,112},{112,0},{1... | collective-permute-start | bytes 786440 | tf_op jit(solution)/shard_map/ppermute | solution.py:296
  162.2 8.7 %collective-permute-start.27 = (bf16[2,32,2048]{2,1,0:T(8,128)(2,1)S(1)}, bf16[2,32,2048]{2,1,0:T(8,128)(2,1)S(1)}, u32[]{:S(2)}, u32[]{:S(2)}) collective-permute-start(bf16[2,32,2048]{2,1,0:T(8,128)(2,1)S(1)} %fusion.1), channel_id=1, source_target_pairs={{0,112},{16,0},{32,16},{48,32},{64,48},{80,64},{96,80},{112,96},{1... | collective-permute-start | bytes 786440 | tf_op jit(solution)/shard_map/ppermute | solution.py:296
  167.6 9.6 %collective-permute-start.15 = (bf16[2,32,2048]{2,1,0:T(8,128)(2,1)S(1)}, bf16[2,32,2048]{2,1,0:T(8,128)(2,1)S(1)}, u32[]{:S(2)}, u32[]{:S(2)}) collective-permute-start(bf16[2,32,2048]{2,1,0:T(8,128)(2,1)S(1)} %fusion.7), channel_id=1, source_target_pairs={{0,16},{16,32},{32,48},{48,64},{64,80},{80,96},{96,112},{112,0},{1... | collective-permute-start | bytes 786440 | tf_op jit(solution)/shard_map/ppermute | solution.py:296
  171.0 7.7 %collective-permute-start.28 = (bf16[2,32,2048]{2,1,0:T(8,128)(2,1)S(1)}, bf16[2,32,2048]{2,1,0:T(8,128)(2,1)S(1)}, u32[]{:S(2)}, u32[]{:S(2)}) collective-permute-start(bf16[2,32,2048]{2,1,0:T(8,128)(2,1)S(1)} %fusion), channel_id=1, source_target_pairs={{0,112},{16,0},{32,16},{48,32},{64,48},{80,64},{96,80},{112,96},{1... | collective-permute-start | bytes 786440 | tf_op jit(solution)/shard_map/ppermute | solution.py:296
  177.4 6.9 %collective-permute-start.19 = (bf16[32,2048]{1,0:T(8,128)(2,1)S(1)}, bf16[32,2048]{1,0:T(8,128)(2,1)S(1)}, u32[]{:S(2)}, u32[]{:S(2)}) collective-permute-start(bf16[32,2048]{1,0:T(8,128)(2,1)S(1)} %dynamic-slice_bitcast_fusion.1), channel_id=1, source_target_pairs={{0,128},{16,144},{32,160},{48,176},{64,192},{80,208},{96,224},{112... | collective-permute-start | bytes 393224 | tf_op jit(solution)/shard_map/ppermute | solution.py:296
  178.7 7.0 %collective-permute-start.29 = (bf16[32,2048]{1,0:T(8,128)(2,1)S(1)}, bf16[32,2048]{1,0:T(8,128)(2,1)S(1)}, u32[]{:S(2)}, u32[]{:S(2)}) collective-permute-start(bf16[32,2048]{1,0:T(8,128)(2,1)S(1)} %dynamic-slice_bitcast_fusion), channel_id=1, source_target_pairs={{0,128},{16,144},{32,160},{48,176},{64,192},{80,208},{96,224},{112... | collective-permute-start | bytes 393224 | tf_op jit(solution)/shard_map/ppermute | solution.py:296
  (11 other events, 102.4 us)
where the time goes:
time: 190 us; the launch traced here: 187 us
  waiting for transfers between devices  81 us (43%)
  starting transfers between devices  60.4 us (32%)
  Pallas kernels  25.6 us (13%)
  local copies, waits for them, and re-layouts  11.3 us (6%)
  other arithmetic  7.53 us (4%)
    ppermute x19, waiting for transfers between devices, move_head(): return lax.ppermute(v, 'head', [(i, f(i)) for i in range(16)])  53.3 us
    ppermute x19, starting transfers between devices, move_head(): return lax.ppermute(v, 'head', [(i, f(i)) for i in range(16)])  34.3 us
    ppermute x11, waiting for transfers between devices, move_ctx(): return lax.ppermute(v, 'ctx', [(i, f(i)) for i in range(16)])  18.5 us
    ppermute x11, starting transfers between devices, move_ctx(): return lax.ppermute(v, 'ctx', [(i, f(i)) for i in range(16)])  15.1 us
    pallas_call x2, Pallas kernels, project(): pl.pallas_call(lambda *refs: project_kernel(hops, *refs), out_shape=[term...  13.7 us
    all_to_all x1, starting transfers between devices, layer(): lax.all_to_all(packed, 'head', split_axis=0, concat_axis=0, tiled=True)  10.9 us
    all_to_all x1, waiting for transfers between devices, layer(): lax.all_to_all(packed, 'head', split_axis=0, concat_axis=0, tiled=True)  9.13 us
    pallas_call x2, Pallas kernels, attend(): pl.pallas_call(lambda *refs: attend_kernel(sets, *refs), out_shape=[part]...  8.58 us
  transfers between devices with their start and end apart: 31, of which 17 were waited for; matrix products, arithmetic and copies ran while one was open for 8% of the time, Pallas kernels for 14%

commit v1 on v0

--- a/solution.py
+++ b/solution.py
@@ -149,7 +149,7 @@
         low = (rest - mid.astype(F32)).astype(BF)
         for p in range(4):
             out_ref[p * HD : (p + 1) * HD, :] = (acc_ref[p * 144 : p * 144 + HD, :] * inv[p : p + 1, :]).astype(BF)
-        out_ref[512:528, :] = jnp.concatenate([hi, mid, low, jnp.zeros((4, 256), BF)], axis=0)
+        out_ref[512:528, :] = jnp.concatenate([hi, mid, low, jnp.ones((4, 256), BF)], axis=0)
 
 
 def attend(sets, flags, bias, lim, qs, kvs):
@@ -199,7 +199,7 @@
     lses = []
     for ref in parts:
         tail = ref[512:528, :].astype(F32)
-        lses.append(tail[0:4] + tail[4:8] + tail[8:12])
+        lses.append(jnp.where(tail[12:16] > 0.5, tail[0:4] + tail[4:8] + tail[8:12], NEG))
     top = jnp.maximum(jnp.maximum(lses[0], lses[1]), jnp.maximum(lses[2], lses[3]))
     ws = [jnp.exp2(lse - top) for lse in lses]
     norm = gate_ref[...] / (ws[0] + ws[1] + ws[2] + ws[3])
@@ -291,6 +291,12 @@
 
     def move_ctx(v, f):
         return lax.ppermute(v, "ctx", [(i, f(i)) for i in range(16)])
+
+    def from_later(v, dx):
+        return lax.ppermute(v, "ctx", [(i, i - NJ * dx) for i in range(NJ * dx, 16)])
+
+    def to_later(v, dx):
+        return lax.ppermute(v, "ctx", [(i, i + NJ * dx) for i in range(16 - NJ * dx)])
 
     def move_head(v, f):
         return lax.ppermute(v, "head", [(i, f(i)) for i in range(16)])
@@ -345,13 +351,14 @@
     earlier_ok = jnp.where(bias[0:4] == 0.0, 127.0, -1.0)
     lim = jnp.where(same[None], in_block[:, None, :], earlier_ok[None]).reshape(16, 256)
 
-    q1 = move_ctx(q_own, lambda i: (i - 4) % 16)
-    q2 = move_ctx(q_own, lambda i: (i - 8) % 16)
-    q3 = move_ctx(q_own, lambda i: (i - 12) % 16)
+    q1, q2, q3 = (from_later(q_own, dx) for dx in (1, 2, 3))
     kv3 = move_ctx(kv2, lambda i: i ^ 1)
     kvs = (kv, kv1, kv2, kv3)
-    parts = attend((1, 2, 3), flags, bias, lim, (q1, q2, q3), kvs)
-    back = [move_ctx(part, lambda i: (i + 4 * dx) % 16) for dx, part in ((1, parts[0]), (2, parts[1]), (3, parts[2]))]
+    back = {}
+    for sets, qs in (((1, 3), (q1, q3)), ((2,), (q2,))):
+        parts = attend(sets, flags, bias, lim, qs, kvs)
+        for dx, part in zip(sets, parts):
+            back[dx] = to_later(part, dx)
     (own,) = attend((0,), flags, bias, lim, (q_own,), kvs)
     sent = pl.pallas_call(
         merge_kernel,
@@ -360,7 +367,7 @@
         out_specs=vmem(),
         compiler_params=grant(8),
         name="merge",
-    )(own, *back, tok, gate)
+    )(own, back[1], back[2], back[3], tok, gate)
     got = move_head(sent, swap)
     w_swapped = []
     for n in range(2):

time: 190 us -> 188 us (0.989)
  the two profiles are of different devices: /device:TPU:4 before, /device:TPU:102 now
where the time goes in v1:
time: 188 us; the launch traced here: 187 us
  waiting for transfers between devices  86.1 us (46%)
  starting transfers between devices  56.8 us (30%)
  Pallas kernels  26.2 us (14%)
  local copies, waits for them, and re-layouts  9.76 us (5%)
  other arithmetic  7.59 us (4%)
    ppermute x19, waiting for transfers between devices, move_head(): return lax.ppermute(v, 'head', [(i, f(i)) for i in range(16)])  57 us
    ppermute x19, starting transfers between devices, move_head(): return lax.ppermute(v, 'head', [(i, f(i)) for i in range(16)])  30.9 us
    ppermute x3, waiting for transfers between devices, to_later(): lax.ppermute(v, 'ctx', [(i, i + NJ * dx) for i in range(16 - NJ * dx)])  17 us
    pallas_call x2, Pallas kernels, project(): pl.pallas_call(lambda *refs: project_kernel(hops, *refs), out_shape=[term...  13.8 us
    ppermute x3, starting transfers between devices, from_later(): lax.ppermute(v, 'ctx', [(i, i - NJ * dx) for i in range(NJ * dx, 16)])  10.4 us
    all_to_all x1, starting transfers between devices, layer(): lax.all_to_all(packed, 'head', split_axis=0, concat_axis=0, tiled=True)  10 us
    pallas_call x3, Pallas kernels, attend(): pl.pallas_call(lambda *refs: attend_kernel(sets, *refs), out_shape=[part]...  8.97 us
    ppermute x5, waiting for transfers between devices, move_ctx(): return lax.ppermute(v, 'ctx', [(i, f(i)) for i in range(16)])  7.19 us
  transfers between devices with their start and end apart: 31, of which 18 were waited for; matrix products, arithmetic and copies ran while one was open for 7% of the time, Pallas kernels for 14%

profile of v1, /device:TPU:102, one launch (start us, length us, event | category | flops | bytes accessed | tf_op | source)
XLA Modules:
  0.0 187.0 jit_solution(2826542198480395608)
XLA Ops:
  6.4 10.0 %all-to-all-start = ((bf16[16,80,128]{2,1,0:T(8,128)(2,1)}), bf16[16,80,128]{2,1,0:T(8,128)(2,1)}, u32[]{:S(2)}, u32[]{:S(2)}) async-start(bf16[16,80,128]{2,1,0:T(8,128)(2,1)} %pack.1), calls=%async_computation | async-start | bytes 655360 | tf_op jit(solution)/shard_map/all_to_all | solution.py:332
  16.4 3.1 %fusion.17 = (bf16[256,2048]{1,0:T(8,128)(2,1)}, bf16[256,2048]{1,0:T(8,128)(2,1)}) fusion(bf16[512,8192]{1,0:T(8,128)(2,1)} %refs_3_.3, s32[]{:T(128)S(6)} %select_n.199, s32[]{:T(128)S(6)} %select_n.200, s32[]{:T(128)S(6)} %select_n.204), kind=kLoop, calls=%fused_computation.76 | loop fusion | bytes 4194316 | tf_op jit(solution)/shard_map/dynamic_slice | solution.py:309
  19.5 3.0 %collective-permute-start.10 = (bf16[256,2048]{1,0:T(8,128)(2,1)}, bf16[256,2048]{1,0:T(8,128)(2,1)}, u32[]{:S(2)}, u32[]{:S(2)}) collective-permute-start(bf16[256,2048]{1,0:T(8,128)(2,1)} %get-tuple-element.29), channel_id=1, source_target_pairs={{0,128},{16,144},{32,160},{48,176},{64,192},{80,208},{96,224},{112... | collective-permute-start | bytes 3145736 | tf_op jit(solution)/shard_map/ppermute | solution.py:302
  24.4 7.2 %collective-permute-done.1.refs_6_.refs_7_ = bf16[1024,512]{1,0:T(8,128)(2,1)S(1)} collective-permute-done((bf16[1024,512]{1,0:T(8,128)(2,1)S(1)}, bf16[1024,512]{1,0:T(8,128)(2,1)S(1)}, u32[]{:S(2)}, u32[]{:S(2)}) %collective-permute-start.1) | collective-permute-done | bytes 1048608 | tf_op jit(solution)/shard_map/ppermute | solution.py:293
  32.4 2.2 %all-to-all-done = bf16[16,80,128]{2,1,0:T(8,128)(2,1)} async-done(((bf16[16,80,128]{2,1,0:T(8,128)(2,1)}), bf16[16,80,128]{2,1,0:T(8,128)(2,1)}, u32[]{:S(2)}, u32[]{:S(2)}) %all-to-all-start) | async-done | bytes 327712 | tf_op jit(solution)/shard_map/all_to_all | solution.py:332
  36.5 4.0 %collective-permute-start.6 = (bf16[16,64,128]{2,1,0:T(8,128)(2,1)S(1)}, bf16[16,64,128]{2,1,0:T(8,128)(2,1)}, u32[]{:S(2)}, u32[]{:S(2)}) collective-permute-start(bf16[16,64,128]{2,1,0:T(8,128)(2,1)S(1)} %slice.75.refs_3_), channel_id=1, source_target_pairs={{8,0},{9,1},{10,2},{11,3},{12,4},{13,5},{14,6},{15,7},{24,16},{25,... | collective-permute-start | bytes 786440 | tf_op jit(solution)/shard_map/ppermute | solution.py:296
  41.9 2.7 %collective-permute-done.6.refs_3_ = bf16[16,64,128]{2,1,0:T(8,128)(2,1)} collective-permute-done((bf16[16,64,128]{2,1,0:T(8,128)(2,1)S(1)}, bf16[16,64,128]{2,1,0:T(8,128)(2,1)}, u32[]{:S(2)}, u32[]{:S(2)}) %collective-permute-start.6) | collective-permute-done | bytes 262176 | tf_op jit(solution)/shard_map/ppermute | solution.py:296
  44.6 2.0 %collective-permute-start.3 = (bf16[16,64,128]{2,1,0:T(8,128)(2,1)S(1)}, bf16[16,64,128]{2,1,0:T(8,128)(2,1)}, u32[]{:S(2)}, u32[]{:S(2)}) collective-permute-start(bf16[16,64,128]{2,1,0:T(8,128)(2,1)S(1)} %slice.75.refs_3_), channel_id=1, source_target_pairs={{4,0},{5,1},{6,2},{7,3},{8,4},{9,5},{10,6},{11,7},{12,8},{13,9},{1... | collective-permute-start | bytes 786440 | tf_op jit(solution)/shard_map/ppermute | solution.py:296
  46.6 4.3 %collective-permute-start.4 = (bf16[16,64,128]{2,1,0:T(8,128)(2,1)S(1)}, bf16[16,64,128]{2,1,0:T(8,128)(2,1)}, u32[]{:S(2)}, u32[]{:S(2)}) collective-permute-start(bf16[16,64,128]{2,1,0:T(8,128)(2,1)S(1)} %slice.75.refs_3_), channel_id=1, source_target_pairs={{12,0},{13,1},{14,2},{15,3},{28,16},{29,17},{30,18},{31,19},{44,32... | collective-permute-start | bytes 786440 | tf_op jit(solution)/shard_map/ppermute | solution.py:296
  50.9 6.2 %collective-permute-done.10.refs_4_ = bf16[256,2048]{1,0:T(8,128)(2,1)} collective-permute-done((bf16[256,2048]{1,0:T(8,128)(2,1)}, bf16[256,2048]{1,0:T(8,128)(2,1)}, u32[]{:S(2)}, u32[]{:S(2)}) %collective-permute-start.10) | collective-permute-done | bytes 1048608 | tf_op jit(solution)/shard_map/ppermute | solution.py:302
  57.1 21.3 %collective-permute-done.20.refs_4_ = bf16[256,2048]{1,0:T(8,128)(2,1)} collective-permute-done((bf16[256,2048]{1,0:T(8,128)(2,1)}, bf16[256,2048]{1,0:T(8,128)(2,1)}, u32[]{:S(2)}, u32[]{:S(2)}) %collective-permute-start.20) | collective-permute-done | bytes 1048608 | tf_op jit(solution)/shard_map/ppermute | solution.py:302
  78.4 3.2 %attend.5 = bf16[528,256]{1,0:T(8,128)(2,1)} custom-call(s32[4,16]{1,0:T(4,128)S(1)} %reshape.178.refs_0_, f32[96,256]{1,0:T(8,128)S(1)} %reshape_reshape.3.refs_1_, f32[16,256]{1,0:T(8,128)S(1)} %select_n.197.refs_2_, bf16[16,64,128]{2,1,0:T(8,128)(2,1)} %collective-permute-done.6.refs_3_, bf16[1024,512]{1,0:T(8,128)(2,1)S(1)} %pad_maximum_fusion.refs_4_.refs_5_, ...), custom_call_target="tpu_custom_call" | custom-call | flops 1073741824 | bytes 5242880 | tf_op jit(solution)/shard_map/attend/pallas_call | solution.py:157
  82.9 3.4 %attend.4 = (bf16[528,256]{1,0:T(8,128)(2,1)}, bf16[528,256]{1,0:T(8,128)(2,1)}) custom-call(s32[4,16]{1,0:T(4,128)S(1)} %reshape.178.refs_0_, f32[96,256]{1,0:T(8,128)S(1)} %reshape_reshape.3.refs_1_, f32[16,256]{1,0:T(8,128)S(1)} %select_n.197.refs_2_, bf16[16,64,128]{2,1,0:T(8,128)(2,1)} %collective-permute-done.3.refs_3_, ...), custom_call_target="tpu_custom_call" | custom-call | flops 2147483648 | bytes 5242880 | tf_op jit(solution)/shard_map/attend/pallas_call | solution.py:157
  89.8 2.4 %attend.3.a_ref = bf16[528,256]{1,0:T(8,128)(2,1)S(1)} custom-call(s32[4,16]{1,0:T(4,128)S(1)} %reshape.178.refs_0_, f32[96,256]{1,0:T(8,128)S(1)} %reshape_reshape.3.refs_1_, f32[16,256]{1,0:T(8,128)S(1)} %select_n.197.refs_2_, bf16[16,64,128]{2,1,0:T(8,128)(2,1)S(1)} %slice.75.refs_3_, bf16[1024,512]{1,0:T(8,128)(2,1)S(1)} %pad_maximum_fusion.refs_4_.refs_5_, ...), custom_call_target="tpu_custom_call" | custom-call | flops 1073741824 | bytes 5242880 | tf_op jit(solution)/shard_map/attend/pallas_call | solution.py:157
  92.2 2.2 %collective-permute-done.7.c_ref = bf16[528,256]{1,0:T(8,128)(2,1)} collective-permute-done((bf16[528,256]{1,0:T(8,128)(2,1)}, bf16[528,256]{1,0:T(8,128)(2,1)}, u32[]{:S(2)}, u32[]{:S(2)}) %collective-permute-start.7) | collective-permute-done | bytes 270368 | tf_op jit(solution)/shard_map/ppermute | solution.py:299
  94.4 4.3 %collective-permute-done.5.b_ref = bf16[528,256]{1,0:T(8,128)(2,1)} collective-permute-done((bf16[528,256]{1,0:T(8,128)(2,1)}, bf16[528,256]{1,0:T(8,128)(2,1)}, u32[]{:S(2)}, u32[]{:S(2)}) %collective-permute-start.5) | collective-permute-done | bytes 270368 | tf_op jit(solution)/shard_map/ppermute | solution.py:299
  98.7 10.5 %collective-permute-done.8.d_ref = bf16[528,256]{1,0:T(8,128)(2,1)} collective-permute-done((bf16[528,256]{1,0:T(8,128)(2,1)}, bf16[528,256]{1,0:T(8,128)(2,1)}, u32[]{:S(2)}, u32[]{:S(2)}) %collective-permute-start.8) | collective-permute-done | bytes 270368 | tf_op jit(solution)/shard_map/ppermute | solution.py:299
  113.2 7.2 %collective-permute-done.9.got_ref = bf16[528,256]{1,0:T(8,128)(2,1)S(1)} collective-permute-done((bf16[528,256]{1,0:T(8,128)(2,1)S(1)}, bf16[528,256]{1,0:T(8,128)(2,1)S(1)}, u32[]{:S(2)}, u32[]{:S(2)}) %collective-permute-start.9) | collective-permute-done | bytes 270368 | tf_op jit(solution)/shard_map/ppermute | solution.py:302
  121.5 6.8 %project.2 = (bf16[2,32,2048]{2,1,0:T(8,128)(2,1)}, bf16[3,2,32,2048]{3,2,1,0:T(8,128)(2,1)}, bf16[2,32,2048]{2,1,0:T(8,128)(2,1)}, bf16[2,2,32,2048]{3,2,1,0:T(8,128)(2,1)}, bf16[2,32,2048]{2,1,0:T(8,128)(2,1)}) custom-call(s32[2]{0:T(128)} %pad_add_fusion.1.refs_0_, bf16[512,512]{1,0:T(8,128)(2,1)} %copy-done, bf16[512,512]{1,0:T(8,128)(2,1)} %copy-done.1, ...), custom_call_target="tpu_custom_call" | custom-call | flops 2147483648 | bytes 7340032 | tf_op jit(solution)/shard_map/project/pallas_call | solution.py:265
  128.4 3.2 %collective-permute-start.12 = (bf16[2,32,2048]{2,1,0:T(8,128)(2,1)}, bf16[2,32,2048]{2,1,0:T(8,128)(2,1)S(1)}, u32[]{:S(2)}, u32[]{:S(2)}) collective-permute-start(bf16[2,32,2048]{2,1,0:T(8,128)(2,1)} %get-tuple-element.20), channel_id=1, source_target_pairs={{0,16},{16,32},{32,48},{48,64},{64,80},{80,96},{96,112},{112,0},{1... | collective-permute-start | bytes 786440 | tf_op jit(solution)/shard_map/ppermute | solution.py:302
  131.6 7.0 %project.3 = (bf16[2,32,2048]{2,1,0:T(8,128)(2,1)}, bf16[2,2,32,2048]{3,2,1,0:T(8,128)(2,1)}, bf16[2,32,2048]{2,1,0:T(8,128)(2,1)}, bf16[3,2,32,2048]{3,2,1,0:T(8,128)(2,1)}, bf16[2,32,2048]{2,1,0:T(8,128)(2,1)}) custom-call(s32[2]{0:T(128)} %pad_add_fusion.1.refs_0_, bf16[512,512]{1,0:T(8,128)(2,1)} %copy-done, bf16[512,512]{1,0:T(8,128)(2,1)} %copy-done.1, ...), custom_call_target="tpu_custom_call" | custom-call | flops 2147483648 | bytes 7340032 | tf_op jit(solution)/shard_map/project/pallas_call | solution.py:265
  138.5 3.2 %collective-permute-start.22 = (bf16[2,32,2048]{2,1,0:T(8,128)(2,1)}, bf16[2,32,2048]{2,1,0:T(8,128)(2,1)S(1)}, u32[]{:S(2)}, u32[]{:S(2)}) collective-permute-start(bf16[2,32,2048]{2,1,0:T(8,128)(2,1)} %get-tuple-element.25), channel_id=1, source_target_pairs={{0,16},{16,32},{32,48},{48,64},{64,80},{80,96},{96,112},{112,0},{1... | collective-permute-start | bytes 786440 | tf_op jit(solution)/shard_map/ppermute | solution.py:302
  141.8 3.3 %collective-permute-start.13 = (bf16[2,32,2048]{2,1,0:T(8,128)(2,1)S(1)}, bf16[2,32,2048]{2,1,0:T(8,128)(2,1)S(1)}, u32[]{:S(2)}, u32[]{:S(2)}) collective-permute-start(bf16[2,32,2048]{2,1,0:T(8,128)(2,1)S(1)} %fusion.9), channel_id=1, source_target_pairs={{0,16},{16,32},{32,48},{48,64},{64,80},{80,96},{96,112},{112,0},{1... | collective-permute-start | bytes 786440 | tf_op jit(solution)/shard_map/ppermute | solution.py:302
  145.3 3.4 %collective-permute-done.22 = bf16[2,32,2048]{2,1,0:T(8,128)(2,1)S(1)} collective-permute-done((bf16[2,32,2048]{2,1,0:T(8,128)(2,1)}, bf16[2,32,2048]{2,1,0:T(8,128)(2,1)S(1)}, u32[]{:S(2)}, u32[]{:S(2)}) %collective-permute-start.22) | collective-permute-done | bytes 262176 | tf_op jit(solution)/shard_map/ppermute | solution.py:302
  149.7 3.7 %collective-permute-start.23 = (bf16[2,32,2048]{2,1,0:T(8,128)(2,1)S(1)}, bf16[2,32,2048]{2,1,0:T(8,128)(2,1)S(1)}, u32[]{:S(2)}, u32[]{:S(2)}) collective-permute-start(bf16[2,32,2048]{2,1,0:T(8,128)(2,1)S(1)} %fusion.4), channel_id=1, source_target_pairs={{0,16},{16,32},{32,48},{48,64},{64,80},{80,96},{96,112},{112,0},{1... | collective-permute-start | bytes 786440 | tf_op jit(solution)/shard_map/ppermute | solution.py:302
  154.3 3.8 %collective-permute-start.14 = (bf16[2,32,2048]{2,1,0:T(8,128)(2,1)S(1)}, bf16[2,32,2048]{2,1,0:T(8,128)(2,1)S(1)}, u32[]{:S(2)}, u32[]{:S(2)}) collective-permute-start(bf16[2,32,2048]{2,1,0:T(8,128)(2,1)S(1)} %fusion.8), channel_id=1, source_target_pairs={{0,16},{16,32},{32,48},{48,64},{64,80},{80,96},{96,112},{112,0},{1... | collective-permute-start | bytes 786440 | tf_op jit(solution)/shard_map/ppermute | solution.py:302
  160.2 3.8 %collective-permute-start.24 = (bf16[2,32,2048]{2,1,0:T(8,128)(2,1)S(1)}, bf16[2,32,2048]{2,1,0:T(8,128)(2,1)S(1)}, u32[]{:S(2)}, u32[]{:S(2)}) collective-permute-start(bf16[2,32,2048]{2,1,0:T(8,128)(2,1)S(1)} %fusion.3), channel_id=1, source_target_pairs={{0,16},{16,32},{32,48},{48,64},{64,80},{80,96},{96,112},{112,0},{1... | collective-permute-start | bytes 786440 | tf_op jit(solution)/shard_map/ppermute | solution.py:302
  165.8 3.8 %collective-permute-start.15 = (bf16[2,32,2048]{2,1,0:T(8,128)(2,1)S(1)}, bf16[2,32,2048]{2,1,0:T(8,128)(2,1)S(1)}, u32[]{:S(2)}, u32[]{:S(2)}) collective-permute-start(bf16[2,32,2048]{2,1,0:T(8,128)(2,1)S(1)} %fusion.7), channel_id=1, source_target_pairs={{0,16},{16,32},{32,48},{48,64},{64,80},{80,96},{96,112},{112,0},{1... | collective-permute-start | bytes 786440 | tf_op jit(solution)/shard_map/ppermute | solution.py:302
  169.5 2.2 %collective-permute-done.27 = bf16[2,32,2048]{2,1,0:T(8,128)(2,1)S(1)} collective-permute-done((bf16[2,32,2048]{2,1,0:T(8,128)(2,1)S(1)}, bf16[2,32,2048]{2,1,0:T(8,128)(2,1)S(1)}, u32[]{:S(2)}, u32[]{:S(2)}) %collective-permute-start.27) | collective-permute-done | bytes 262176 | tf_op jit(solution)/shard_map/ppermute | solution.py:302
  171.9 2.0 %collective-permute-done.15 = bf16[2,32,2048]{2,1,0:T(8,128)(2,1)S(1)} collective-permute-done((bf16[2,32,2048]{2,1,0:T(8,128)(2,1)S(1)}, bf16[2,32,2048]{2,1,0:T(8,128)(2,1)S(1)}, u32[]{:S(2)}, u32[]{:S(2)}) %collective-permute-start.15) | collective-permute-done | bytes 262176 | tf_op jit(solution)/shard_map/ppermute | solution.py:302
  174.8 4.7 %collective-permute-done.28 = bf16[2,32,2048]{2,1,0:T(8,128)(2,1)S(1)} collective-permute-done((bf16[2,32,2048]{2,1,0:T(8,128)(2,1)S(1)}, bf16[2,32,2048]{2,1,0:T(8,128)(2,1)S(1)}, u32[]{:S(2)}, u32[]{:S(2)}) %collective-permute-start.28) | collective-permute-done | bytes 262176 | tf_op jit(solution)/shard_map/ppermute | solution.py:302
  182.0 4.2 %collective-permute-done.29 = bf16[32,2048]{1,0:T(8,128)(2,1)S(1)} collective-permute-done((bf16[32,2048]{1,0:T(8,128)(2,1)S(1)}, bf16[32,2048]{1,0:T(8,128)(2,1)S(1)}, u32[]{:S(2)}, u32[]{:S(2)}) %collective-permute-start.29) | collective-permute-done | bytes 131104 | tf_op jit(solution)/shard_map/ppermute | solution.py:302
  (130 shorter events, 32.3 us)
Async XLA Ops:
  2.4 29.2 %collective-permute-start.1 = (bf16[1024,512]{1,0:T(8,128)(2,1)S(1)}, bf16[1024,512]{1,0:T(8,128)(2,1)S(1)}, u32[]{:S(2)}, u32[]{:S(2)}) collective-permute-start(bf16[1024,512]{1,0:T(8,128)(2,1)S(1)} %pad_maximum_fusion.refs_4_.refs_5_), channel_id=1, source_target_pairs={{0,2},{1,3},{2,0},{3,1},{4,6},{5,7},{6,4},{7,5},{8,10},{9,11},{10,... | collective-permute-start | bytes 3145736 | tf_op jit(solution)/shard_map/ppermute | solution.py:293
  4.1 42.5 %collective-permute-start = (bf16[1024,512]{1,0:T(8,128)(2,1)S(1)}, bf16[1024,512]{1,0:T(8,128)(2,1)S(1)}, u32[]{:S(2)}, u32[]{:S(2)}) collective-permute-start(bf16[1024,512]{1,0:T(8,128)(2,1)S(1)} %pad_maximum_fusion.refs_4_.refs_5_), channel_id=1, source_target_pairs={{0,1},{1,0},{2,3},{3,2},{4,5},{5,4},{6,7},{7,6},{8,9},{9,8},{10,11... | collective-permute-start | bytes 3145736 | tf_op jit(solution)/shard_map/ppermute | solution.py:293
  6.4 28.2 %all-to-all-start = ((bf16[16,80,128]{2,1,0:T(8,128)(2,1)}), bf16[16,80,128]{2,1,0:T(8,128)(2,1)}, u32[]{:S(2)}, u32[]{:S(2)}) async-start(bf16[16,80,128]{2,1,0:T(8,128)(2,1)} %pack.1), calls=%async_computation | async-start | bytes 655360 | tf_op jit(solution)/shard_map/all_to_all | solution.py:332
  19.5 37.6 %collective-permute-start.10 = (bf16[256,2048]{1,0:T(8,128)(2,1)}, bf16[256,2048]{1,0:T(8,128)(2,1)}, u32[]{:S(2)}, u32[]{:S(2)}) collective-permute-start(bf16[256,2048]{1,0:T(8,128)(2,1)} %get-tuple-element.29), channel_id=1, source_target_pairs={{0,128},{16,144},{32,160},{48,176},{64,192},{80,208},{96,224},{112... | collective-permute-start | bytes 3145736 | tf_op jit(solution)/shard_map/ppermute | solution.py:302
  22.5 55.9 %collective-permute-start.20 = (bf16[256,2048]{1,0:T(8,128)(2,1)}, bf16[256,2048]{1,0:T(8,128)(2,1)}, u32[]{:S(2)}, u32[]{:S(2)}) collective-permute-start(bf16[256,2048]{1,0:T(8,128)(2,1)} %get-tuple-element.30), channel_id=1, source_target_pairs={{0,128},{16,144},{32,160},{48,176},{64,192},{80,208},{96,224},{112... | collective-permute-start | bytes 3145736 | tf_op jit(solution)/shard_map/ppermute | solution.py:302
  31.6 46.8 %collective-permute-start.2 = (bf16[1024,512]{1,0:T(8,128)(2,1)S(1)}, bf16[1024,512]{1,0:T(8,128)(2,1)}, u32[]{:S(2)}, u32[]{:S(2)}) collective-permute-start(bf16[1024,512]{1,0:T(8,128)(2,1)S(1)} %collective-permute-done.1.refs_6_.refs_7_), channel_id=1, source_target_pairs={{0,1},{1,0},{2,3},{3,2},{4,5},{5,4},{6,7},{7,6},{8,9},{9,8},{10,11... | collective-permute-start | bytes 3145736 | tf_op jit(solution)/shard_map/ppermute | solution.py:293
  36.5 8.1 %collective-permute-start.6 = (bf16[16,64,128]{2,1,0:T(8,128)(2,1)S(1)}, bf16[16,64,128]{2,1,0:T(8,128)(2,1)}, u32[]{:S(2)}, u32[]{:S(2)}) collective-permute-start(bf16[16,64,128]{2,1,0:T(8,128)(2,1)S(1)} %slice.75.refs_3_), channel_id=1, source_target_pairs={{8,0},{9,1},{10,2},{11,3},{12,4},{13,5},{14,6},{15,7},{24,16},{25,... | collective-permute-start | bytes 786440 | tf_op jit(solution)/shard_map/ppermute | solution.py:296
  44.6 38.3 %collective-permute-start.3 = (bf16[16,64,128]{2,1,0:T(8,128)(2,1)S(1)}, bf16[16,64,128]{2,1,0:T(8,128)(2,1)}, u32[]{:S(2)}, u32[]{:S(2)}) collective-permute-start(bf16[16,64,128]{2,1,0:T(8,128)(2,1)S(1)} %slice.75.refs_3_), channel_id=1, source_target_pairs={{4,0},{5,1},{6,2},{7,3},{8,4},{9,5},{10,6},{11,7},{12,8},{13,9},{1... | collective-permute-start | bytes 786440 | tf_op jit(solution)/shard_map/ppermute | solution.py:296
  46.6 36.3 %collective-permute-start.4 = (bf16[16,64,128]{2,1,0:T(8,128)(2,1)S(1)}, bf16[16,64,128]{2,1,0:T(8,128)(2,1)}, u32[]{:S(2)}, u32[]{:S(2)}) collective-permute-start(bf16[16,64,128]{2,1,0:T(8,128)(2,1)S(1)} %slice.75.refs_3_), channel_id=1, source_target_pairs={{12,0},{13,1},{14,2},{15,3},{28,16},{29,17},{30,18},{31,19},{44,32... | collective-permute-start | bytes 786440 | tf_op jit(solution)/shard_map/ppermute | solution.py:296
  57.1 64.4 %collective-permute-start.11 = (bf16[256,2048]{1,0:T(8,128)(2,1)}, bf16[256,2048]{1,0:T(8,128)(2,1)}, u32[]{:S(2)}, u32[]{:S(2)}) collective-permute-start(bf16[256,2048]{1,0:T(8,128)(2,1)} %collective-permute-done.10.refs_4_), channel_id=1, source_target_pairs={{0,1},{1,0},{2,3},{3,2},{4,5},{5,4},{6,7},{7,6},{8,9},{9,8},{10,11... | collective-permute-start | bytes 3145736 | tf_op jit(solution)/shard_map/ppermute | solution.py:293
  78.4 53.1 %collective-permute-start.21 = (bf16[256,2048]{1,0:T(8,128)(2,1)}, bf16[256,2048]{1,0:T(8,128)(2,1)}, u32[]{:S(2)}, u32[]{:S(2)}) collective-permute-start(bf16[256,2048]{1,0:T(8,128)(2,1)} %collective-permute-done.20.refs_4_), channel_id=1, source_target_pairs={{0,1},{1,0},{2,3},{3,2},{4,5},{5,4},{6,7},{7,6},{8,9},{9,8},{10,11... | collective-permute-start | bytes 3145736 | tf_op jit(solution)/shard_map/ppermute | solution.py:293
  81.6 12.7 %collective-permute-start.7 = (bf16[528,256]{1,0:T(8,128)(2,1)}, bf16[528,256]{1,0:T(8,128)(2,1)}, u32[]{:S(2)}, u32[]{:S(2)}) collective-permute-start(bf16[528,256]{1,0:T(8,128)(2,1)} %attend.5), channel_id=1, source_target_pairs={{0,8},{1,9},{2,10},{3,11},{4,12},{5,13},{6,14},{7,15},{16,24},{17,... | collective-permute-start | bytes 811016 | tf_op jit(solution)/shard_map/ppermute | solution.py:299
  86.3 12.4 %collective-permute-start.5 = (bf16[528,256]{1,0:T(8,128)(2,1)}, bf16[528,256]{1,0:T(8,128)(2,1)}, u32[]{:S(2)}, u32[]{:S(2)}) collective-permute-start(bf16[528,256]{1,0:T(8,128)(2,1)} %get-tuple-element.17), channel_id=1, source_target_pairs={{0,4},{1,5},{2,6},{3,7},{4,8},{5,9},{6,10},{7,11},{8,12},{9,13},{1... | collective-permute-start | bytes 811016 | tf_op jit(solution)/shard_map/ppermute | solution.py:299
  87.6 21.6 %collective-permute-start.8 = (bf16[528,256]{1,0:T(8,128)(2,1)}, bf16[528,256]{1,0:T(8,128)(2,1)}, u32[]{:S(2)}, u32[]{:S(2)}) collective-permute-start(bf16[528,256]{1,0:T(8,128)(2,1)} %get-tuple-element.18), channel_id=1, source_target_pairs={{0,12},{1,13},{2,14},{3,15},{16,28},{17,29},{18,30},{19,31},{32,44... | collective-permute-start | bytes 811016 | tf_op jit(solution)/shard_map/ppermute | solution.py:299
  110.6 9.8 %collective-permute-start.9 = (bf16[528,256]{1,0:T(8,128)(2,1)S(1)}, bf16[528,256]{1,0:T(8,128)(2,1)S(1)}, u32[]{:S(2)}, u32[]{:S(2)}) collective-permute-start(bf16[528,256]{1,0:T(8,128)(2,1)S(1)} %merge.1.sent_ref), channel_id=1, source_target_pairs={{0,128},{16,144},{32,160},{48,176},{64,192},{80,208},{96,224},{112... | collective-permute-start | bytes 811016 | tf_op jit(solution)/shard_map/ppermute | solution.py:302
  128.4 13.3 %collective-permute-start.12 = (bf16[2,32,2048]{2,1,0:T(8,128)(2,1)}, bf16[2,32,2048]{2,1,0:T(8,128)(2,1)S(1)}, u32[]{:S(2)}, u32[]{:S(2)}) collective-permute-start(bf16[2,32,2048]{2,1,0:T(8,128)(2,1)} %get-tuple-element.20), channel_id=1, source_target_pairs={{0,16},{16,32},{32,48},{48,64},{64,80},{80,96},{96,112},{112,0},{1... | collective-permute-start | bytes 786440 | tf_op jit(solution)/shard_map/ppermute | solution.py:302
  131.5 13.5 %collective-permute-start.16 = (bf16[2,32,2048]{2,1,0:T(8,128)(2,1)}, bf16[2,32,2048]{2,1,0:T(8,128)(2,1)S(1)}, u32[]{:S(2)}, u32[]{:S(2)}) collective-permute-start(bf16[2,32,2048]{2,1,0:T(8,128)(2,1)} %get-tuple-element.22), channel_id=1, source_target_pairs={{0,112},{16,0},{32,16},{48,32},{64,48},{80,64},{96,80},{112,96},{1... | collective-permute-start | bytes 786440 | tf_op jit(solution)/shard_map/ppermute | solution.py:302
  138.5 10.2 %collective-permute-start.22 = (bf16[2,32,2048]{2,1,0:T(8,128)(2,1)}, bf16[2,32,2048]{2,1,0:T(8,128)(2,1)S(1)}, u32[]{:S(2)}, u32[]{:S(2)}) collective-permute-start(bf16[2,32,2048]{2,1,0:T(8,128)(2,1)} %get-tuple-element.25), channel_id=1, source_target_pairs={{0,16},{16,32},{32,48},{48,64},{64,80},{80,96},{96,112},{112,0},{1... | collective-permute-start | bytes 786440 | tf_op jit(solution)/shard_map/ppermute | solution.py:302
  141.7 11.7 %collective-permute-start.25 = (bf16[2,32,2048]{2,1,0:T(8,128)(2,1)}, bf16[2,32,2048]{2,1,0:T(8,128)(2,1)S(1)}, u32[]{:S(2)}, u32[]{:S(2)}) collective-permute-start(bf16[2,32,2048]{2,1,0:T(8,128)(2,1)} %get-tuple-element.27), channel_id=1, source_target_pairs={{0,112},{16,0},{32,16},{48,32},{64,48},{80,64},{96,80},{112,96},{1... | collective-permute-start | bytes 786440 | tf_op jit(solution)/shard_map/ppermute | solution.py:302
  141.8 12.4 %collective-permute-start.13 = (bf16[2,32,2048]{2,1,0:T(8,128)(2,1)S(1)}, bf16[2,32,2048]{2,1,0:T(8,128)(2,1)S(1)}, u32[]{:S(2)}, u32[]{:S(2)}) collective-permute-start(bf16[2,32,2048]{2,1,0:T(8,128)(2,1)S(1)} %fusion.9), channel_id=1, source_target_pairs={{0,16},{16,32},{32,48},{48,64},{64,80},{80,96},{96,112},{112,0},{1... | collective-permute-start | bytes 786440 | tf_op jit(solution)/shard_map/ppermute | solution.py:302
  145.2 12.9 %collective-permute-start.17 = (bf16[2,32,2048]{2,1,0:T(8,128)(2,1)S(1)}, bf16[2,32,2048]{2,1,0:T(8,128)(2,1)S(1)}, u32[]{:S(2)}, u32[]{:S(2)}) collective-permute-start(bf16[2,32,2048]{2,1,0:T(8,128)(2,1)S(1)} %fusion.6), channel_id=1, source_target_pairs={{0,112},{16,0},{32,16},{48,32},{64,48},{80,64},{96,80},{112,96},{1... | collective-permute-start | bytes 786440 | tf_op jit(solution)/shard_map/ppermute | solution.py:302
  149.7 10.4 %collective-permute-start.23 = (bf16[2,32,2048]{2,1,0:T(8,128)(2,1)S(1)}, bf16[2,32,2048]{2,1,0:T(8,128)(2,1)S(1)}, u32[]{:S(2)}, u32[]{:S(2)}) collective-permute-start(bf16[2,32,2048]{2,1,0:T(8,128)(2,1)S(1)} %fusion.4), channel_id=1, source_target_pairs={{0,16},{16,32},{32,48},{48,64},{64,80},{80,96},{96,112},{112,0},{1... | collective-permute-start | bytes 786440 | tf_op jit(solution)/shard_map/ppermute | solution.py:302
  153.5 10.5 %collective-permute-start.26 = (bf16[2,32,2048]{2,1,0:T(8,128)(2,1)S(1)}, bf16[2,32,2048]{2,1,0:T(8,128)(2,1)S(1)}, u32[]{:S(2)}, u32[]{:S(2)}) collective-permute-start(bf16[2,32,2048]{2,1,0:T(8,128)(2,1)S(1)} %fusion.2), channel_id=1, source_target_pairs={{0,112},{16,0},{32,16},{48,32},{64,48},{80,64},{96,80},{112,96},{1... | collective-permute-start | bytes 786440 | tf_op jit(solution)/shard_map/ppermute | solution.py:302
  154.3 11.4 %collective-permute-start.14 = (bf16[2,32,2048]{2,1,0:T(8,128)(2,1)S(1)}, bf16[2,32,2048]{2,1,0:T(8,128)(2,1)S(1)}, u32[]{:S(2)}, u32[]{:S(2)}) collective-permute-start(bf16[2,32,2048]{2,1,0:T(8,128)(2,1)S(1)} %fusion.8), channel_id=1, source_target_pairs={{0,16},{16,32},{32,48},{48,64},{64,80},{80,96},{96,112},{112,0},{1... | collective-permute-start | bytes 786440 | tf_op jit(solution)/shard_map/ppermute | solution.py:302
  158.1 21.4 %copy-start.8 = (bf16[2,32,2048]{2,1,0:T(8,128)(2,1)S(1)}, bf16[2,32,2048]{2,1,0:T(8,128)(2,1)}, u32[]{:S(2)}) copy-start(bf16[2,32,2048]{2,1,0:T(8,128)(2,1)} %get-tuple-element.24) | copy-start | bytes 786436
  158.2 13.8 %collective-permute-start.18 = (bf16[2,32,2048]{2,1,0:T(8,128)(2,1)S(1)}, bf16[2,32,2048]{2,1,0:T(8,128)(2,1)S(1)}, u32[]{:S(2)}, u32[]{:S(2)}) collective-permute-start(bf16[2,32,2048]{2,1,0:T(8,128)(2,1)S(1)} %fusion.5), channel_id=1, source_target_pairs={{0,112},{16,0},{32,16},{48,32},{64,48},{80,64},{96,80},{112,96},{1... | collective-permute-start | bytes 786440 | tf_op jit(solution)/shard_map/ppermute | solution.py:302
  160.2 14.7 %collective-permute-start.24 = (bf16[2,32,2048]{2,1,0:T(8,128)(2,1)S(1)}, bf16[2,32,2048]{2,1,0:T(8,128)(2,1)S(1)}, u32[]{:S(2)}, u32[]{:S(2)}) collective-permute-start(bf16[2,32,2048]{2,1,0:T(8,128)(2,1)S(1)} %fusion.3), channel_id=1, source_target_pairs={{0,16},{16,32},{32,48},{48,64},{64,80},{80,96},{96,112},{112,0},{1... | collective-permute-start | bytes 786440 | tf_op jit(solution)/shard_map/ppermute | solution.py:302
  164.0 7.8 %collective-permute-start.27 = (bf16[2,32,2048]{2,1,0:T(8,128)(2,1)S(1)}, bf16[2,32,2048]{2,1,0:T(8,128)(2,1)S(1)}, u32[]{:S(2)}, u32[]{:S(2)}) collective-permute-start(bf16[2,32,2048]{2,1,0:T(8,128)(2,1)S(1)} %fusion.1), channel_id=1, source_target_pairs={{0,112},{16,0},{32,16},{48,32},{64,48},{80,64},{96,80},{112,96},{1... | collective-permute-start | bytes 786440 | tf_op jit(solution)/shard_map/ppermute | solution.py:302
  165.8 8.2 %collective-permute-start.15 = (bf16[2,32,2048]{2,1,0:T(8,128)(2,1)S(1)}, bf16[2,32,2048]{2,1,0:T(8,128)(2,1)S(1)}, u32[]{:S(2)}, u32[]{:S(2)}) collective-permute-start(bf16[2,32,2048]{2,1,0:T(8,128)(2,1)S(1)} %fusion.7), channel_id=1, source_target_pairs={{0,16},{16,32},{32,48},{48,64},{64,80},{80,96},{96,112},{112,0},{1... | collective-permute-start | bytes 786440 | tf_op jit(solution)/shard_map/ppermute | solution.py:302
  171.8 7.7 %collective-permute-start.28 = (bf16[2,32,2048]{2,1,0:T(8,128)(2,1)S(1)}, bf16[2,32,2048]{2,1,0:T(8,128)(2,1)S(1)}, u32[]{:S(2)}, u32[]{:S(2)}) collective-permute-start(bf16[2,32,2048]{2,1,0:T(8,128)(2,1)S(1)} %fusion), channel_id=1, source_target_pairs={{0,112},{16,0},{32,16},{48,32},{64,48},{80,64},{96,80},{112,96},{1... | collective-permute-start | bytes 786440 | tf_op jit(solution)/shard_map/ppermute | solution.py:302
  174.1 7.8 %collective-permute-start.19 = (bf16[32,2048]{1,0:T(8,128)(2,1)S(1)}, bf16[32,2048]{1,0:T(8,128)(2,1)S(1)}, u32[]{:S(2)}, u32[]{:S(2)}) collective-permute-start(bf16[32,2048]{1,0:T(8,128)(2,1)S(1)} %dynamic-slice_bitcast_fusion.1), channel_id=1, source_target_pairs={{0,128},{16,144},{32,160},{48,176},{64,192},{80,208},{96,224},{112... | collective-permute-start | bytes 393224 | tf_op jit(solution)/shard_map/ppermute | solution.py:302
  179.6 6.6 %collective-permute-start.29 = (bf16[32,2048]{1,0:T(8,128)(2,1)S(1)}, bf16[32,2048]{1,0:T(8,128)(2,1)S(1)}, u32[]{:S(2)}, u32[]{:S(2)}) collective-permute-start(bf16[32,2048]{1,0:T(8,128)(2,1)S(1)} %dynamic-slice_bitcast_fusion), channel_id=1, source_target_pairs={{0,128},{16,144},{32,160},{48,176},{64,192},{80,208},{96,224},{112... | collective-permute-start | bytes 393224 | tf_op jit(solution)/shard_map/ppermute | solution.py:302
  (11 other events, 98.7 us)

commit v2 on v1

--- a/solution.py
+++ b/solution.py
@@ -49,12 +49,17 @@
 
 def attend_kernel(sets, flag_ref, bias_ref, lim_ref, *refs):
     count = len(sets)
-    q_refs, kv_refs, out_refs = refs[:count], refs[count : count + 4], refs[count + 4 : 2 * count + 4]
-    kv, sems, list_ref, done_ref, s_ref, m_ref, acc_ref = refs[2 * count + 4 :]
-    copies = [pltpu.make_async_copy(src, kv.at[i], sems.at[i]) for i, src in enumerate(kv_refs)]
+    q_refs, kv_refs, out_refs = refs[:count], refs[count : count + 8], refs[count + 8 : 2 * count + 8]
+    kv, sems, list_ref, done_ref, s_ref, m_ref, acc_ref = refs[2 * count + 8 :]
+    copies = []
+    for i in range(4):
+        for n in range(2):
+            part = kv.at[i, n * 512 : (n + 1) * 512]
+            copies.append(pltpu.make_async_copy(kv_refs[i * 2 + n], part, sems.at[i * 2 + n]))
     for copy in copies:
         copy.start()
     copies[0].wait()
+    copies[1].wait()
     done_ref[0] = jnp.int32(0)
 
     def keys_ready(last):
@@ -62,7 +67,8 @@
 
             @pl.when((last >= i) & (done_ref[0] < i))
             def _():
-                copies[i].wait()
+                copies[2 * i].wait()
+                copies[2 * i + 1].wait()
                 done_ref[0] = jnp.int32(i)
 
     ones = jnp.ones((16, 256), BF)
@@ -159,11 +165,11 @@
         out_shape=[part] * len(sets),
         in_specs=[pl.BlockSpec(memory_space=pltpu.SMEM)]
         + [vmem()] * (2 + len(sets))
-        + [pl.BlockSpec(memory_space=pl.ANY)] * 4,
+        + [pl.BlockSpec(memory_space=pl.ANY)] * 8,
         out_specs=[vmem()] * len(sets),
         scratch_shapes=[
             pltpu.VMEM((4, 1024, 512), BF),
-            pltpu.SemaphoreType.DMA((4,)),
+            pltpu.SemaphoreType.DMA((8,)),
             pltpu.SMEM((18,), jnp.int32),
             pltpu.SMEM((1,), jnp.int32),
             pltpu.VMEM((4, 256, 256), F32),
@@ -213,15 +219,15 @@
     send_ref[512:528, :] = jnp.concatenate([tok_ref[...], jnp.zeros((12, 256), F32)], axis=0).astype(BF)
 
 
-def place_kernel(sent_ref, out_ref):
+def place_kernel(at_ref, sent_ref, out_ref):
     pos = slot_pos(sent_ref[512:528, :].astype(F32))
     for p in range(4):
         place_heads(sent_ref[p * HD : (p + 1) * HD, :], pos[p : p + 1, :], out_ref, p * HD)
 
 
-def spread_kernel(core_ref, got_ref, out_ref):
+def spread_kernel(at_ref, got_ref, out_ref):
     pos = slot_pos(got_ref[512:528, :].astype(F32))
-    core = core_ref[0]
+    core = at_ref[2]
     for n in range(4):
         half = core if n < 2 else 1 - core
         q = n % 2
@@ -278,6 +284,7 @@
             out_specs=[block(*lead) for lead in leads],
             scratch_shapes=[pltpu.VMEM((512, TILE), BF)],
         ),
+        compiler_params=grant(56),
         cost_estimate=pl.CostEstimate(flops=2 * 512 * 1024 * HALF, bytes_accessed=7 << 20, transcendentals=0),
         name="project",
     )(place, a, b, w_out, wb, wc)
@@ -309,9 +316,12 @@
         given = lax.dynamic_slice(w_out, ((ctx % 2) * 256, (2 * (1 - y) + n) * HALF), (256, HALF))
         w_fetched.append(move_head(given, swap))
 
-    kv = jnp.concatenate([keys, values.T], axis=0)
-    kv2 = move_ctx(kv, lambda i: i ^ 2)
-    kv1 = move_ctx(kv, lambda i: i ^ 1)
+    def partners(v):
+        return move_ctx(v, lambda i: i ^ 2), move_ctx(v, lambda i: i ^ 1)
+
+    turned = values.T
+    k2, k1 = partners(keys)
+    v2, v1 = partners(turned)
 
     head_ids = jnp.arange(H, dtype=jnp.int32)
     onehot = (routes[:, :, None] == head_ids[None, None, :]).astype(F32)
@@ -326,7 +336,6 @@
         out_shape=jax.ShapeDtypeStruct((16, 80, HD), BF),
         in_specs=[vmem()] * 3,
         out_specs=vmem(),
-        compiler_params=grant(12),
         name="pack",
     )(queries, target, gate_row)
     arrived = lax.all_to_all(packed, "head", split_axis=0, concat_axis=0, tiled=True)
@@ -352,8 +361,8 @@
     lim = jnp.where(same[None], in_block[:, None, :], earlier_ok[None]).reshape(16, 256)
 
     q1, q2, q3 = (from_later(q_own, dx) for dx in (1, 2, 3))
-    kv3 = move_ctx(kv2, lambda i: i ^ 1)
-    kvs = (kv, kv1, kv2, kv3)
+    k3, v3 = move_ctx(k2, lambda i: i ^ 1), move_ctx(v2, lambda i: i ^ 1)
+    kvs = (keys, turned, k1, v1, k2, v2, k3, v3)
     back = {}
     for sets, qs in (((1, 3), (q1, q3)), ((2,), (q2,))):
         parts = attend(sets, flags, bias, lim, qs, kvs)
@@ -373,9 +382,10 @@
     for n in range(2):
         w_swapped.append(move_ctx(w_fetched[n], lambda i: i ^ 1))
     tokens = jax.ShapeDtypeStruct((512, 512), BF)
+    at = jnp.stack([y, z, ctx % 2])
     mine = pl.pallas_call(
-        place_kernel, out_shape=tokens, in_specs=[vmem()], out_specs=vmem(), compiler_params=grant(8), name="place"
-    )(sent)
+        place_kernel, out_shape=tokens, in_specs=[pl.BlockSpec(memory_space=pltpu.SMEM), vmem()], out_specs=vmem(), compiler_params=grant(8), name="place"
+    )(at, sent)
     theirs = pl.pallas_call(
         spread_kernel,
         out_shape=tokens,
@@ -383,16 +393,14 @@
         out_specs=vmem(),
         compiler_params=grant(8),
         name="spread",
-    )((ctx % 2).reshape(1), got)
+    )(at, got)
 
     def shift(step):
         return lambda i: (i // NZ) * NZ + (i % NZ + step) % NZ
 
     here, there = [], []
     for chunk, hops in ((0, (4, 3)), (1, (3, 4))):
-        up0, up, down0, down, total = project(
-            jnp.stack([y, z]), chunk, hops, mine, theirs, w_out, w_fetched[chunk], w_swapped[chunk]
-        )
+        up0, up, down0, down, total = project(at, chunk, hops, mine, theirs, w_out, w_fetched[chunk], w_swapped[chunk])
         total = total.astype(F32)
         for step, length, message, rest in ((1, hops[0], up0, up), (-1, hops[1], down0, down)):
             for hop in range(length):

time: 188 us -> 191 us (1.016)
  the two profiles are of different devices: /device:TPU:102 before, /device:TPU:98 now
where the time goes in v2:
time: 191 us; the launch traced here: 190 us
  waiting for transfers between devices  77.4 us (41%)
  starting transfers between devices  53.6 us (28%)
  Pallas kernels  35.1 us (18%)
  local copies, waits for them, and re-layouts  12.3 us (6%)
  other arithmetic  10.5 us (5%)
    ppermute x19, waiting for transfers between devices, move_head(): return lax.ppermute(v, 'head', [(i, f(i)) for i in range(16)])  55.1 us
    ppermute x19, starting transfers between devices, move_head(): return lax.ppermute(v, 'head', [(i, f(i)) for i in range(16)])  30.3 us
    pallas_call x3, Pallas kernels, attend(): pl.pallas_call(lambda *refs: attend_kernel(sets, *refs), out_shape=[part]...  15.9 us
    pallas_call x2, Pallas kernels, project(): pl.pallas_call(lambda *refs: project_kernel(hops, *refs), out_shape=[term...  13.9 us
    all_to_all x1, starting transfers between devices, layer(): lax.all_to_all(packed, 'head', split_axis=0, concat_axis=0, tiled=True)  10.3 us
    ppermute x3, waiting for transfers between devices, from_later(): lax.ppermute(v, 'ctx', [(i, i - NJ * dx) for i in range(NJ * dx, 16)])  9.51 us
    ppermute x3, waiting for transfers between devices, to_later(): lax.ppermute(v, 'ctx', [(i, i + NJ * dx) for i in range(16 - NJ * dx)])  8.68 us
    ppermute x3, starting transfers between devices, to_later(): lax.ppermute(v, 'ctx', [(i, i + NJ * dx) for i in range(16 - NJ * dx)])  5.48 us
  transfers between devices with their start and end apart: 34, of which 11 were waited for; matrix products, arithmetic and copies ran while one was open for 10% of the time, Pallas kernels for 19%

profile of v2, /device:TPU:98, one launch (start us, length us, event | category | flops | bytes accessed | tf_op | source)
XLA Modules:
  0.0 189.6 jit_solution(8229142353261151846)
XLA Ops:
  1.3 1.7 collective-permute-start.3
  7.1 2.3 %pack.1 = bf16[16,80,128]{2,1,0:T(8,128)(2,1)} custom-call(bf16[32,2048]{1,0:T(8,128)(2,1)} %q_ref.1, s32[1,512]{1,0:T(1,128)} %reshape.171.tgt_ref, f32[1,512]{1,0:T(1,128)} %reshape.172.gate_ref), custom_call_target="tpu_custom_call" | custom-call | tf_op jit(solution)/shard_map/pack/pallas_call | solution.py:334
  9.4 10.3 %all-to-all-start = ((bf16[16,80,128]{2,1,0:T(8,128)(2,1)}), bf16[16,80,128]{2,1,0:T(8,128)(2,1)}, u32[]{:S(2)}, u32[]{:S(2)}) async-start(bf16[16,80,128]{2,1,0:T(8,128)(2,1)} %pack.1), calls=%async_computation | async-start | bytes 655360 | tf_op jit(solution)/shard_map/all_to_all | solution.py:341
  19.7 3.1 %fusion.17 = (bf16[256,2048]{1,0:T(8,128)(2,1)}, bf16[256,2048]{1,0:T(8,128)(2,1)}) fusion(bf16[512,8192]{1,0:T(8,128)(2,1)} %refs_3_.3, s32[]{:T(128)S(6)} %select_n.199, s32[]{:T(128)S(6)} %select_n.200, s32[]{:T(128)S(6)} %select_n.204), kind=kLoop, calls=%fused_computation.75 | loop fusion | bytes 4194316 | tf_op jit(solution)/shard_map/dynamic_slice | solution.py:316
  22.8 3.0 %collective-permute-start.13 = (bf16[256,2048]{1,0:T(8,128)(2,1)}, bf16[256,2048]{1,0:T(8,128)(2,1)}, u32[]{:S(2)}, u32[]{:S(2)}) collective-permute-start(bf16[256,2048]{1,0:T(8,128)(2,1)} %get-tuple-element.29), channel_id=1, source_target_pairs={{0,128},{16,144},{32,160},{48,176},{64,192},{80,208},{96,224},{112... | collective-permute-start | bytes 3145736 | tf_op jit(solution)/shard_map/ppermute | solution.py:309
  29.3 4.2 %all-to-all-done = bf16[16,80,128]{2,1,0:T(8,128)(2,1)} async-done(((bf16[16,80,128]{2,1,0:T(8,128)(2,1)}), bf16[16,80,128]{2,1,0:T(8,128)(2,1)}, u32[]{:S(2)}, u32[]{:S(2)}) %all-to-all-start) | async-done | bytes 327712 | tf_op jit(solution)/shard_map/all_to_all | solution.py:341
  38.2 9.5 %collective-permute-done.9.refs_3_ = bf16[16,64,128]{2,1,0:T(8,128)(2,1)} collective-permute-done((bf16[16,64,128]{2,1,0:T(8,128)(2,1)S(1)}, bf16[16,64,128]{2,1,0:T(8,128)(2,1)}, u32[]{:S(2)}, u32[]{:S(2)}) %collective-permute-start.9) | collective-permute-done | bytes 262176 | tf_op jit(solution)/shard_map/ppermute | solution.py:303
  47.7 2.4 %collective-permute-start.6 = (bf16[16,64,128]{2,1,0:T(8,128)(2,1)S(1)}, bf16[16,64,128]{2,1,0:T(8,128)(2,1)}, u32[]{:S(2)}, u32[]{:S(2)}) collective-permute-start(bf16[16,64,128]{2,1,0:T(8,128)(2,1)S(1)} %slice.75.refs_3_), channel_id=1, source_target_pairs={{4,0},{5,1},{6,2},{7,3},{8,4},{9,5},{10,6},{11,7},{12,8},{13,9},{1... | collective-permute-start | bytes 786440 | tf_op jit(solution)/shard_map/ppermute | solution.py:303
  51.6 4.4 %collective-permute-done.13.refs_4_ = bf16[256,2048]{1,0:T(8,128)(2,1)} collective-permute-done((bf16[256,2048]{1,0:T(8,128)(2,1)}, bf16[256,2048]{1,0:T(8,128)(2,1)}, u32[]{:S(2)}, u32[]{:S(2)}) %collective-permute-start.13) | collective-permute-done | bytes 1048608 | tf_op jit(solution)/shard_map/ppermute | solution.py:309
  56.0 21.3 %collective-permute-done.23.refs_4_ = bf16[256,2048]{1,0:T(8,128)(2,1)} collective-permute-done((bf16[256,2048]{1,0:T(8,128)(2,1)}, bf16[256,2048]{1,0:T(8,128)(2,1)}, u32[]{:S(2)}, u32[]{:S(2)}) %collective-permute-start.23) | collective-permute-done | bytes 1048608 | tf_op jit(solution)/shard_map/ppermute | solution.py:309
  77.3 5.8 %attend.5 = bf16[528,256]{1,0:T(8,128)(2,1)} custom-call(s32[4,16]{1,0:T(4,128)S(1)} %reshape.174.refs_0_, f32[96,256]{1,0:T(8,128)S(1)} %reshape_reshape.3.refs_1_, f32[16,256]{1,0:T(8,128)S(1)} %select_n.198.refs_2_, bf16[16,64,128]{2,1,0:T(8,128)(2,1)} %collective-permute-done.9.refs_3_, bf16[512,512]{1,0:T(8,128)(2,1)S(1)} %copy-done.2, ...), custom_call_target="tpu_custom_call" | custom-call | flops 1073741824 | bytes 5242880 | tf_op jit(solution)/shard_map/attend/pallas_call | solution.py:163
  83.1 2.2 %collective-permute-start.10 = (bf16[528,256]{1,0:T(8,128)(2,1)}, bf16[528,256]{1,0:T(8,128)(2,1)}, u32[]{:S(2)}, u32[]{:S(2)}) collective-permute-start(bf16[528,256]{1,0:T(8,128)(2,1)} %attend.5), channel_id=1, source_target_pairs={{0,8},{1,9},{2,10},{3,11},{4,12},{5,13},{6,14},{7,15},{16,24},{17,... | collective-permute-start | bytes 811016 | tf_op jit(solution)/shard_map/ppermute | solution.py:306
  85.3 7.5 %attend.4 = (bf16[528,256]{1,0:T(8,128)(2,1)}, bf16[528,256]{1,0:T(8,128)(2,1)}) custom-call(s32[4,16]{1,0:T(4,128)S(1)} %reshape.174.refs_0_, f32[96,256]{1,0:T(8,128)S(1)} %reshape_reshape.3.refs_1_, f32[16,256]{1,0:T(8,128)S(1)} %select_n.198.refs_2_, bf16[16,64,128]{2,1,0:T(8,128)(2,1)} %collective-permute-done.6.refs_3_, ...), custom_call_target="tpu_custom_call" | custom-call | flops 2147483648 | bytes 5242880 | tf_op jit(solution)/shard_map/attend/pallas_call | solution.py:163
  92.8 1.4 collective-permute-start.11
  94.2 1.9 %collective-permute-start.8 = (bf16[528,256]{1,0:T(8,128)(2,1)}, bf16[528,256]{1,0:T(8,128)(2,1)}, u32[]{:S(2)}, u32[]{:S(2)}) collective-permute-start(bf16[528,256]{1,0:T(8,128)(2,1)} %get-tuple-element.17), channel_id=1, source_target_pairs={{0,4},{1,5},{2,6},{3,7},{4,8},{5,9},{6,10},{7,11},{8,12},{9,13},{1... | collective-permute-start | bytes 811016 | tf_op jit(solution)/shard_map/ppermute | solution.py:306
  96.9 2.6 %attend.3.a_ref = bf16[528,256]{1,0:T(8,128)(2,1)S(1)} custom-call(s32[4,16]{1,0:T(4,128)S(1)} %reshape.174.refs_0_, f32[96,256]{1,0:T(8,128)S(1)} %reshape_reshape.3.refs_1_, f32[16,256]{1,0:T(8,128)S(1)} %select_n.198.refs_2_, bf16[16,64,128]{2,1,0:T(8,128)(2,1)S(1)} %slice.75.refs_3_, bf16[512,512]{1,0:T(8,128)(2,1)S(1)} %copy-done.2, ...), custom_call_target="tpu_custom_call" | custom-call | flops 1073741824 | bytes 5242880 | tf_op jit(solution)/shard_map/attend/pallas_call | solution.py:163
  99.6 8.7 %collective-permute-done.8.b_ref = bf16[528,256]{1,0:T(8,128)(2,1)} collective-permute-done((bf16[528,256]{1,0:T(8,128)(2,1)}, bf16[528,256]{1,0:T(8,128)(2,1)}, u32[]{:S(2)}, u32[]{:S(2)}) %collective-permute-start.8) | collective-permute-done | bytes 270368 | tf_op jit(solution)/shard_map/ppermute | solution.py:306
  112.0 7.2 %collective-permute-done.12.got_ref = bf16[528,256]{1,0:T(8,128)(2,1)S(1)} collective-permute-done((bf16[528,256]{1,0:T(8,128)(2,1)S(1)}, bf16[528,256]{1,0:T(8,128)(2,1)S(1)}, u32[]{:S(2)}, u32[]{:S(2)}) %collective-permute-start.12) | collective-permute-done | bytes 270368 | tf_op jit(solution)/shard_map/ppermute | solution.py:309
  120.9 6.9 %project.2 = (bf16[2,32,2048]{2,1,0:T(8,128)(2,1)}, bf16[3,2,32,2048]{3,2,1,0:T(8,128)(2,1)}, bf16[2,32,2048]{2,1,0:T(8,128)(2,1)}, bf16[2,2,32,2048]{3,2,1,0:T(8,128)(2,1)}, bf16[2,32,2048]{2,1,0:T(8,128)(2,1)}) custom-call(s32[3]{0:T(128)} %copy-done.3, bf16[512,512]{1,0:T(8,128)(2,1)} %copy-done, bf16[512,512]{1,0:T(8,128)(2,1)} %copy-done.1, ...), custom_call_target="tpu_custom_call" | custom-call | flops 2147483648 | bytes 7340032 | tf_op jit(solution)/shard_map/project/pallas_call | solution.py:271
  127.8 3.2 %collective-permute-start.15 = (bf16[2,32,2048]{2,1,0:T(8,128)(2,1)}, bf16[2,32,2048]{2,1,0:T(8,128)(2,1)S(1)}, u32[]{:S(2)}, u32[]{:S(2)}) collective-permute-start(bf16[2,32,2048]{2,1,0:T(8,128)(2,1)} %get-tuple-element.20), channel_id=1, source_target_pairs={{0,16},{16,32},{32,48},{48,64},{64,80},{80,96},{96,112},{112,0},{1... | collective-permute-start | bytes 786440 | tf_op jit(solution)/shard_map/ppermute | solution.py:309
  131.0 7.0 %project.3 = (bf16[2,32,2048]{2,1,0:T(8,128)(2,1)}, bf16[2,2,32,2048]{3,2,1,0:T(8,128)(2,1)}, bf16[2,32,2048]{2,1,0:T(8,128)(2,1)}, bf16[3,2,32,2048]{3,2,1,0:T(8,128)(2,1)}, bf16[2,32,2048]{2,1,0:T(8,128)(2,1)}) custom-call(s32[3]{0:T(128)} %copy-done.3, bf16[512,512]{1,0:T(8,128)(2,1)} %copy-done, bf16[512,512]{1,0:T(8,128)(2,1)} %copy-done.1, ...), custom_call_target="tpu_custom_call" | custom-call | flops 2147483648 | bytes 7340032 | tf_op jit(solution)/shard_map/project/pallas_call | solution.py:271
  138.0 3.2 %collective-permute-start.25 = (bf16[2,32,2048]{2,1,0:T(8,128)(2,1)}, bf16[2,32,2048]{2,1,0:T(8,128)(2,1)S(1)}, u32[]{:S(2)}, u32[]{:S(2)}) collective-permute-start(bf16[2,32,2048]{2,1,0:T(8,128)(2,1)} %get-tuple-element.25), channel_id=1, source_target_pairs={{0,16},{16,32},{32,48},{48,64},{64,80},{80,96},{96,112},{112,0},{1... | collective-permute-start | bytes 786440 | tf_op jit(solution)/shard_map/ppermute | solution.py:309
  141.3 3.3 %collective-permute-start.16 = (bf16[2,32,2048]{2,1,0:T(8,128)(2,1)S(1)}, bf16[2,32,2048]{2,1,0:T(8,128)(2,1)S(1)}, u32[]{:S(2)}, u32[]{:S(2)}) collective-permute-start(bf16[2,32,2048]{2,1,0:T(8,128)(2,1)S(1)} %fusion.9), channel_id=1, source_target_pairs={{0,16},{16,32},{32,48},{48,64},{64,80},{80,96},{96,112},{112,0},{1... | collective-permute-start | bytes 786440 | tf_op jit(solution)/shard_map/ppermute | solution.py:309
  144.7 3.5 %collective-permute-done.25 = bf16[2,32,2048]{2,1,0:T(8,128)(2,1)S(1)} collective-permute-done((bf16[2,32,2048]{2,1,0:T(8,128)(2,1)}, bf16[2,32,2048]{2,1,0:T(8,128)(2,1)S(1)}, u32[]{:S(2)}, u32[]{:S(2)}) %collective-permute-start.25) | collective-permute-done | bytes 262176 | tf_op jit(solution)/shard_map/ppermute | solution.py:309
  149.2 3.7 %collective-permute-start.26 = (bf16[2,32,2048]{2,1,0:T(8,128)(2,1)S(1)}, bf16[2,32,2048]{2,1,0:T(8,128)(2,1)S(1)}, u32[]{:S(2)}, u32[]{:S(2)}) collective-permute-start(bf16[2,32,2048]{2,1,0:T(8,128)(2,1)S(1)} %fusion.4), channel_id=1, source_target_pairs={{0,16},{16,32},{32,48},{48,64},{64,80},{80,96},{96,112},{112,0},{1... | collective-permute-start | bytes 786440 | tf_op jit(solution)/shard_map/ppermute | solution.py:309
  154.1 3.5 %collective-permute-start.17 = (bf16[2,32,2048]{2,1,0:T(8,128)(2,1)S(1)}, bf16[2,32,2048]{2,1,0:T(8,128)(2,1)S(1)}, u32[]{:S(2)}, u32[]{:S(2)}) collective-permute-start(bf16[2,32,2048]{2,1,0:T(8,128)(2,1)S(1)} %fusion.8), channel_id=1, source_target_pairs={{0,16},{16,32},{32,48},{48,64},{64,80},{80,96},{96,112},{112,0},{1... | collective-permute-start | bytes 786440 | tf_op jit(solution)/shard_map/ppermute | solution.py:309
  157.7 1.9 collective-permute-done.26
  160.6 3.8 %collective-permute-start.27 = (bf16[2,32,2048]{2,1,0:T(8,128)(2,1)S(1)}, bf16[2,32,2048]{2,1,0:T(8,128)(2,1)S(1)}, u32[]{:S(2)}, u32[]{:S(2)}) collective-permute-start(bf16[2,32,2048]{2,1,0:T(8,128)(2,1)S(1)} %fusion.3), channel_id=1, source_target_pairs={{0,16},{16,32},{32,48},{48,64},{64,80},{80,96},{96,112},{112,0},{1... | collective-permute-start | bytes 786440 | tf_op jit(solution)/shard_map/ppermute | solution.py:309
  165.8 3.3 %collective-permute-start.18 = (bf16[2,32,2048]{2,1,0:T(8,128)(2,1)S(1)}, bf16[2,32,2048]{2,1,0:T(8,128)(2,1)S(1)}, u32[]{:S(2)}, u32[]{:S(2)}) collective-permute-start(bf16[2,32,2048]{2,1,0:T(8,128)(2,1)S(1)} %fusion.7), channel_id=1, source_target_pairs={{0,16},{16,32},{32,48},{48,64},{64,80},{80,96},{96,112},{112,0},{1... | collective-permute-start | bytes 786440 | tf_op jit(solution)/shard_map/ppermute | solution.py:309
  169.1 4.3 %collective-permute-done.30 = bf16[2,32,2048]{2,1,0:T(8,128)(2,1)S(1)} collective-permute-done((bf16[2,32,2048]{2,1,0:T(8,128)(2,1)S(1)}, bf16[2,32,2048]{2,1,0:T(8,128)(2,1)S(1)}, u32[]{:S(2)}, u32[]{:S(2)}) %collective-permute-start.30) | collective-permute-done | bytes 262176 | tf_op jit(solution)/shard_map/ppermute | solution.py:309
  175.4 6.7 %collective-permute-done.31 = bf16[2,32,2048]{2,1,0:T(8,128)(2,1)S(1)} collective-permute-done((bf16[2,32,2048]{2,1,0:T(8,128)(2,1)S(1)}, bf16[2,32,2048]{2,1,0:T(8,128)(2,1)S(1)}, u32[]{:S(2)}, u32[]{:S(2)}) %collective-permute-start.31) | collective-permute-done | bytes 262176 | tf_op jit(solution)/shard_map/ppermute | solution.py:309
  183.0 5.8 %collective-permute-done.32 = bf16[32,2048]{1,0:T(8,128)(2,1)S(1)} collective-permute-done((bf16[32,2048]{1,0:T(8,128)(2,1)S(1)}, bf16[32,2048]{1,0:T(8,128)(2,1)S(1)}, u32[]{:S(2)}, u32[]{:S(2)}) %collective-permute-start.32) | collective-permute-done | bytes 131104 | tf_op jit(solution)/shard_map/ppermute | solution.py:309
  (127 shorter events, 29.8 us)
Async XLA Ops:
  1.3 26.6 %collective-permute-start.3 = (bf16[512,512]{1,0:T(8,128)(2,1)S(1)}, bf16[512,512]{1,0:T(8,128)(2,1)S(1)}, u32[]{:S(2)}, u32[]{:S(2)}) collective-permute-start(bf16[512,512]{1,0:T(8,128)(2,1)S(1)} %bitcast.65), channel_id=1, source_target_pairs={{0,2},{1,3},{2,0},{3,1},{4,6},{5,7},{6,4},{7,5},{8,10},{9,11},{10,... | collective-permute-start | bytes 1572872 | tf_op jit(solution)/shard_map/ppermute | solution.py:300
  3.0 26.3 %collective-permute-start.1 = (bf16[512,512]{1,0:T(8,128)(2,1)S(1)}, bf16[512,512]{1,0:T(8,128)(2,1)S(1)}, u32[]{:S(2)}, u32[]{:S(2)}) collective-permute-start(bf16[512,512]{1,0:T(8,128)(2,1)S(1)} %bitcast.66), channel_id=1, source_target_pairs={{0,1},{1,0},{2,3},{3,2},{4,5},{5,4},{6,7},{7,6},{8,9},{9,8},{10,11... | collective-permute-start | bytes 1572872 | tf_op jit(solution)/shard_map/ppermute | solution.py:300
  3.0 32.4 %collective-permute-start.2 = (bf16[512,512]{1,0:T(8,128)(2,1)}, bf16[512,512]{1,0:T(8,128)(2,1)S(1)}, u32[]{:S(2)}, u32[]{:S(2)}) collective-permute-start(bf16[512,512]{1,0:T(8,128)(2,1)} %refs_4_.3), channel_id=1, source_target_pairs={{0,2},{1,3},{2,0},{3,1},{4,6},{5,7},{6,4},{7,5},{8,10},{9,11},{10,... | collective-permute-start | bytes 1572872 | tf_op jit(solution)/shard_map/ppermute | solution.py:300
  3.4 32.1 %collective-permute-start = (bf16[512,512]{1,0:T(8,128)(2,1)}, bf16[512,512]{1,0:T(8,128)(2,1)S(1)}, u32[]{:S(2)}, u32[]{:S(2)}) collective-permute-start(bf16[512,512]{1,0:T(8,128)(2,1)} %refs_4_.3), channel_id=1, source_target_pairs={{0,1},{1,0},{2,3},{3,2},{4,5},{5,4},{6,7},{7,6},{8,9},{9,8},{10,11... | collective-permute-start | bytes 1572872 | tf_op jit(solution)/shard_map/ppermute | solution.py:300
  9.4 24.1 %all-to-all-start = ((bf16[16,80,128]{2,1,0:T(8,128)(2,1)}), bf16[16,80,128]{2,1,0:T(8,128)(2,1)}, u32[]{:S(2)}, u32[]{:S(2)}) async-start(bf16[16,80,128]{2,1,0:T(8,128)(2,1)} %pack.1), calls=%async_computation | async-start | bytes 655360 | tf_op jit(solution)/shard_map/all_to_all | solution.py:341
  22.8 33.2 %collective-permute-start.13 = (bf16[256,2048]{1,0:T(8,128)(2,1)}, bf16[256,2048]{1,0:T(8,128)(2,1)}, u32[]{:S(2)}, u32[]{:S(2)}) collective-permute-start(bf16[256,2048]{1,0:T(8,128)(2,1)} %get-tuple-element.29), channel_id=1, source_target_pairs={{0,128},{16,144},{32,160},{48,176},{64,192},{80,208},{96,224},{112... | collective-permute-start | bytes 3145736 | tf_op jit(solution)/shard_map/ppermute | solution.py:309
  27.9 49.4 %collective-permute-start.23 = (bf16[256,2048]{1,0:T(8,128)(2,1)}, bf16[256,2048]{1,0:T(8,128)(2,1)}, u32[]{:S(2)}, u32[]{:S(2)}) collective-permute-start(bf16[256,2048]{1,0:T(8,128)(2,1)} %get-tuple-element.30), channel_id=1, source_target_pairs={{0,128},{16,144},{32,160},{48,176},{64,192},{80,208},{96,224},{112... | collective-permute-start | bytes 3145736 | tf_op jit(solution)/shard_map/ppermute | solution.py:309
  29.3 20.9 %collective-permute-start.5 = (bf16[512,512]{1,0:T(8,128)(2,1)S(1)}, bf16[512,512]{1,0:T(8,128)(2,1)}, u32[]{:S(2)}, u32[]{:S(2)}) collective-permute-start(bf16[512,512]{1,0:T(8,128)(2,1)S(1)} %collective-permute-done.3.refs_9_.refs_10_), channel_id=1, source_target_pairs={{0,1},{1,0},{2,3},{3,2},{4,5},{5,4},{6,7},{7,6},{8,9},{9,8},{10,11... | collective-permute-start | bytes 1572872 | tf_op jit(solution)/shard_map/ppermute | solution.py:300
  35.4 41.9 %collective-permute-start.4 = (bf16[512,512]{1,0:T(8,128)(2,1)S(1)}, bf16[512,512]{1,0:T(8,128)(2,1)}, u32[]{:S(2)}, u32[]{:S(2)}) collective-permute-start(bf16[512,512]{1,0:T(8,128)(2,1)S(1)} %collective-permute-done.2.refs_8_.refs_9_), channel_id=1, source_target_pairs={{0,1},{1,0},{2,3},{3,2},{4,5},{5,4},{6,7},{7,6},{8,9},{9,8},{10,11... | collective-permute-start | bytes 1572872 | tf_op jit(solution)/shard_map/ppermute | solution.py:300
  35.5 12.2 %collective-permute-start.9 = (bf16[16,64,128]{2,1,0:T(8,128)(2,1)S(1)}, bf16[16,64,128]{2,1,0:T(8,128)(2,1)}, u32[]{:S(2)}, u32[]{:S(2)}) collective-permute-start(bf16[16,64,128]{2,1,0:T(8,128)(2,1)S(1)} %slice.75.refs_3_), channel_id=1, source_target_pairs={{8,0},{9,1},{10,2},{11,3},{12,4},{13,5},{14,6},{15,7},{24,16},{25,... | collective-permute-start | bytes 786440 | tf_op jit(solution)/shard_map/ppermute | solution.py:303
  47.7 37.6 %collective-permute-start.6 = (bf16[16,64,128]{2,1,0:T(8,128)(2,1)S(1)}, bf16[16,64,128]{2,1,0:T(8,128)(2,1)}, u32[]{:S(2)}, u32[]{:S(2)}) collective-permute-start(bf16[16,64,128]{2,1,0:T(8,128)(2,1)S(1)} %slice.75.refs_3_), channel_id=1, source_target_pairs={{4,0},{5,1},{6,2},{7,3},{8,4},{9,5},{10,6},{11,7},{12,8},{13,9},{1... | collective-permute-start | bytes 786440 | tf_op jit(solution)/shard_map/ppermute | solution.py:303
  50.2 35.1 %collective-permute-start.7 = (bf16[16,64,128]{2,1,0:T(8,128)(2,1)S(1)}, bf16[16,64,128]{2,1,0:T(8,128)(2,1)}, u32[]{:S(2)}, u32[]{:S(2)}) collective-permute-start(bf16[16,64,128]{2,1,0:T(8,128)(2,1)S(1)} %slice.75.refs_3_), channel_id=1, source_target_pairs={{12,0},{13,1},{14,2},{15,3},{28,16},{29,17},{30,18},{31,19},{44,32... | collective-permute-start | bytes 786440 | tf_op jit(solution)/shard_map/ppermute | solution.py:303
  56.0 64.9 %collective-permute-start.14 = (bf16[256,2048]{1,0:T(8,128)(2,1)}, bf16[256,2048]{1,0:T(8,128)(2,1)}, u32[]{:S(2)}, u32[]{:S(2)}) collective-permute-start(bf16[256,2048]{1,0:T(8,128)(2,1)} %collective-permute-done.13.refs_4_), channel_id=1, source_target_pairs={{0,1},{1,0},{2,3},{3,2},{4,5},{5,4},{6,7},{7,6},{8,9},{9,8},{10,11... | collective-permute-start | bytes 3145736 | tf_op jit(solution)/shard_map/ppermute | solution.py:300
  77.3 53.7 %collective-permute-start.24 = (bf16[256,2048]{1,0:T(8,128)(2,1)}, bf16[256,2048]{1,0:T(8,128)(2,1)}, u32[]{:S(2)}, u32[]{:S(2)}) collective-permute-start(bf16[256,2048]{1,0:T(8,128)(2,1)} %collective-permute-done.23.refs_4_), channel_id=1, source_target_pairs={{0,1},{1,0},{2,3},{3,2},{4,5},{5,4},{6,7},{7,6},{8,9},{9,8},{10,11... | collective-permute-start | bytes 3145736 | tf_op jit(solution)/shard_map/ppermute | solution.py:300
  83.1 16.4 %collective-permute-start.10 = (bf16[528,256]{1,0:T(8,128)(2,1)}, bf16[528,256]{1,0:T(8,128)(2,1)}, u32[]{:S(2)}, u32[]{:S(2)}) collective-permute-start(bf16[528,256]{1,0:T(8,128)(2,1)} %attend.5), channel_id=1, source_target_pairs={{0,8},{1,9},{2,10},{3,11},{4,12},{5,13},{6,14},{7,15},{16,24},{17,... | collective-permute-start | bytes 811016 | tf_op jit(solution)/shard_map/ppermute | solution.py:306
  94.2 14.1 %collective-permute-start.8 = (bf16[528,256]{1,0:T(8,128)(2,1)}, bf16[528,256]{1,0:T(8,128)(2,1)}, u32[]{:S(2)}, u32[]{:S(2)}) collective-permute-start(bf16[528,256]{1,0:T(8,128)(2,1)} %get-tuple-element.17), channel_id=1, source_target_pairs={{0,4},{1,5},{2,6},{3,7},{4,8},{5,9},{6,10},{7,11},{8,12},{9,13},{1... | collective-permute-start | bytes 811016 | tf_op jit(solution)/shard_map/ppermute | solution.py:306
  109.6 9.6 %collective-permute-start.12 = (bf16[528,256]{1,0:T(8,128)(2,1)S(1)}, bf16[528,256]{1,0:T(8,128)(2,1)S(1)}, u32[]{:S(2)}, u32[]{:S(2)}) collective-permute-start(bf16[528,256]{1,0:T(8,128)(2,1)S(1)} %merge.1.sent_ref), channel_id=1, source_target_pairs={{0,128},{16,144},{32,160},{48,176},{64,192},{80,208},{96,224},{112... | collective-permute-start | bytes 811016 | tf_op jit(solution)/shard_map/ppermute | solution.py:309
  127.8 13.4 %collective-permute-start.15 = (bf16[2,32,2048]{2,1,0:T(8,128)(2,1)}, bf16[2,32,2048]{2,1,0:T(8,128)(2,1)S(1)}, u32[]{:S(2)}, u32[]{:S(2)}) collective-permute-start(bf16[2,32,2048]{2,1,0:T(8,128)(2,1)} %get-tuple-element.20), channel_id=1, source_target_pairs={{0,16},{16,32},{32,48},{48,64},{64,80},{80,96},{96,112},{112,0},{1... | collective-permute-start | bytes 786440 | tf_op jit(solution)/shard_map/ppermute | solution.py:309
  131.0 13.6 %collective-permute-start.19 = (bf16[2,32,2048]{2,1,0:T(8,128)(2,1)}, bf16[2,32,2048]{2,1,0:T(8,128)(2,1)S(1)}, u32[]{:S(2)}, u32[]{:S(2)}) collective-permute-start(bf16[2,32,2048]{2,1,0:T(8,128)(2,1)} %get-tuple-element.22), channel_id=1, source_target_pairs={{0,112},{16,0},{32,16},{48,32},{64,48},{80,64},{96,80},{112,96},{1... | collective-permute-start | bytes 786440 | tf_op jit(solution)/shard_map/ppermute | solution.py:309
  138.0 10.2 %collective-permute-start.25 = (bf16[2,32,2048]{2,1,0:T(8,128)(2,1)}, bf16[2,32,2048]{2,1,0:T(8,128)(2,1)S(1)}, u32[]{:S(2)}, u32[]{:S(2)}) collective-permute-start(bf16[2,32,2048]{2,1,0:T(8,128)(2,1)} %get-tuple-element.25), channel_id=1, source_target_pairs={{0,16},{16,32},{32,48},{48,64},{64,80},{80,96},{96,112},{112,0},{1... | collective-permute-start | bytes 786440 | tf_op jit(solution)/shard_map/ppermute | solution.py:309
  141.2 11.7 %collective-permute-start.28 = (bf16[2,32,2048]{2,1,0:T(8,128)(2,1)}, bf16[2,32,2048]{2,1,0:T(8,128)(2,1)S(1)}, u32[]{:S(2)}, u32[]{:S(2)}) collective-permute-start(bf16[2,32,2048]{2,1,0:T(8,128)(2,1)} %get-tuple-element.27), channel_id=1, source_target_pairs={{0,112},{16,0},{32,16},{48,32},{64,48},{80,64},{96,80},{112,96},{1... | collective-permute-start | bytes 786440 | tf_op jit(solution)/shard_map/ppermute | solution.py:309
  141.3 12.7 %collective-permute-start.16 = (bf16[2,32,2048]{2,1,0:T(8,128)(2,1)S(1)}, bf16[2,32,2048]{2,1,0:T(8,128)(2,1)S(1)}, u32[]{:S(2)}, u32[]{:S(2)}) collective-permute-start(bf16[2,32,2048]{2,1,0:T(8,128)(2,1)S(1)} %fusion.9), channel_id=1, source_target_pairs={{0,16},{16,32},{32,48},{48,64},{64,80},{80,96},{96,112},{112,0},{1... | collective-permute-start | bytes 786440 | tf_op jit(solution)/shard_map/ppermute | solution.py:309
  144.6 12.9 %collective-permute-start.20 = (bf16[2,32,2048]{2,1,0:T(8,128)(2,1)S(1)}, bf16[2,32,2048]{2,1,0:T(8,128)(2,1)S(1)}, u32[]{:S(2)}, u32[]{:S(2)}) collective-permute-start(bf16[2,32,2048]{2,1,0:T(8,128)(2,1)S(1)} %fusion.6), channel_id=1, source_target_pairs={{0,112},{16,0},{32,16},{48,32},{64,48},{80,64},{96,80},{112,96},{1... | collective-permute-start | bytes 786440 | tf_op jit(solution)/shard_map/ppermute | solution.py:309
  149.2 10.4 %collective-permute-start.26 = (bf16[2,32,2048]{2,1,0:T(8,128)(2,1)S(1)}, bf16[2,32,2048]{2,1,0:T(8,128)(2,1)S(1)}, u32[]{:S(2)}, u32[]{:S(2)}) collective-permute-start(bf16[2,32,2048]{2,1,0:T(8,128)(2,1)S(1)} %fusion.4), channel_id=1, source_target_pairs={{0,16},{16,32},{32,48},{48,64},{64,80},{80,96},{96,112},{112,0},{1... | collective-permute-start | bytes 786440 | tf_op jit(solution)/shard_map/ppermute | solution.py:309
  153.9 10.5 %collective-permute-start.29 = (bf16[2,32,2048]{2,1,0:T(8,128)(2,1)S(1)}, bf16[2,32,2048]{2,1,0:T(8,128)(2,1)S(1)}, u32[]{:S(2)}, u32[]{:S(2)}) collective-permute-start(bf16[2,32,2048]{2,1,0:T(8,128)(2,1)S(1)} %fusion.2), channel_id=1, source_target_pairs={{0,112},{16,0},{32,16},{48,32},{64,48},{80,64},{96,80},{112,96},{1... | collective-permute-start | bytes 786440 | tf_op jit(solution)/shard_map/ppermute | solution.py:309
  154.1 11.6 %collective-permute-start.17 = (bf16[2,32,2048]{2,1,0:T(8,128)(2,1)S(1)}, bf16[2,32,2048]{2,1,0:T(8,128)(2,1)S(1)}, u32[]{:S(2)}, u32[]{:S(2)}) collective-permute-start(bf16[2,32,2048]{2,1,0:T(8,128)(2,1)S(1)} %fusion.8), channel_id=1, source_target_pairs={{0,16},{16,32},{32,48},{48,64},{64,80},{80,96},{96,112},{112,0},{1... | collective-permute-start | bytes 786440 | tf_op jit(solution)/shard_map/ppermute | solution.py:309
  157.6 16.9 %collective-permute-start.21 = (bf16[2,32,2048]{2,1,0:T(8,128)(2,1)S(1)}, bf16[2,32,2048]{2,1,0:T(8,128)(2,1)S(1)}, u32[]{:S(2)}, u32[]{:S(2)}) collective-permute-start(bf16[2,32,2048]{2,1,0:T(8,128)(2,1)S(1)} %fusion.5), channel_id=1, source_target_pairs={{0,112},{16,0},{32,16},{48,32},{64,48},{80,64},{96,80},{112,96},{1... | collective-permute-start | bytes 786440 | tf_op jit(solution)/shard_map/ppermute | solution.py:309
  160.6 14.8 %collective-permute-start.27 = (bf16[2,32,2048]{2,1,0:T(8,128)(2,1)S(1)}, bf16[2,32,2048]{2,1,0:T(8,128)(2,1)S(1)}, u32[]{:S(2)}, u32[]{:S(2)}) collective-permute-start(bf16[2,32,2048]{2,1,0:T(8,128)(2,1)S(1)} %fusion.3), channel_id=1, source_target_pairs={{0,16},{16,32},{32,48},{48,64},{64,80},{80,96},{96,112},{112,0},{1... | collective-permute-start | bytes 786440 | tf_op jit(solution)/shard_map/ppermute | solution.py:309
  165.4 8.0 %collective-permute-start.30 = (bf16[2,32,2048]{2,1,0:T(8,128)(2,1)S(1)}, bf16[2,32,2048]{2,1,0:T(8,128)(2,1)S(1)}, u32[]{:S(2)}, u32[]{:S(2)}) collective-permute-start(bf16[2,32,2048]{2,1,0:T(8,128)(2,1)S(1)} %fusion.1), channel_id=1, source_target_pairs={{0,112},{16,0},{32,16},{48,32},{64,48},{80,64},{96,80},{112,96},{1... | collective-permute-start | bytes 786440 | tf_op jit(solution)/shard_map/ppermute | solution.py:309
  165.8 8.7 %collective-permute-start.18 = (bf16[2,32,2048]{2,1,0:T(8,128)(2,1)S(1)}, bf16[2,32,2048]{2,1,0:T(8,128)(2,1)S(1)}, u32[]{:S(2)}, u32[]{:S(2)}) collective-permute-start(bf16[2,32,2048]{2,1,0:T(8,128)(2,1)S(1)} %fusion.7), channel_id=1, source_target_pairs={{0,16},{16,32},{32,48},{48,64},{64,80},{80,96},{96,112},{112,0},{1... | collective-permute-start | bytes 786440 | tf_op jit(solution)/shard_map/ppermute | solution.py:309
  174.4 7.7 %collective-permute-start.31 = (bf16[2,32,2048]{2,1,0:T(8,128)(2,1)S(1)}, bf16[2,32,2048]{2,1,0:T(8,128)(2,1)S(1)}, u32[]{:S(2)}, u32[]{:S(2)}) collective-permute-start(bf16[2,32,2048]{2,1,0:T(8,128)(2,1)S(1)} %fusion), channel_id=1, source_target_pairs={{0,112},{16,0},{32,16},{48,32},{64,48},{80,64},{96,80},{112,96},{1... | collective-permute-start | bytes 786440 | tf_op jit(solution)/shard_map/ppermute | solution.py:309
  174.7 8.3 %collective-permute-start.22 = (bf16[32,2048]{1,0:T(8,128)(2,1)S(1)}, bf16[32,2048]{1,0:T(8,128)(2,1)S(1)}, u32[]{:S(2)}, u32[]{:S(2)}) collective-permute-start(bf16[32,2048]{1,0:T(8,128)(2,1)S(1)} %dynamic-slice_bitcast_fusion.1), channel_id=1, source_target_pairs={{0,128},{16,144},{32,160},{48,176},{64,192},{80,208},{96,224},{112... | collective-permute-start | bytes 393224 | tf_op jit(solution)/shard_map/ppermute | solution.py:309
  (10 other events, 220.5 us)
